TPU v7x, 512 devices: a whole 4x4x16 slice. The times are simulated.
512 devices in a mesh: src: 32 (over z, x_lo), rcv: 8 (over y, x_hi), frq: 2 (over core).
Axes of the slice: x: 4 (x_hi: 2, x_lo: 2; x = x_hi * 2 + x_lo), y: 4, z: 16, core: 2. Of those that a mesh axis runs over, the one named last changes fastest.
Arguments:
- f_time: bfloat16 [512, 64, 8192], P('frq', 'src', 'rcv'), may hold values from -6 to 6
- reflect: bfloat16 [2, 8, 5888, 8192], P(None, 'frq', 'src', 'rcv'), may hold values from -0.0625 to 0.0625
- band_map: int32 [736, 32], P('src', 'rcv'), may hold values from 0 to 1, as said below
- gates: int32 [64], replicated, may hold values from 128 to 511
Outputs:
- focused: bfloat16 [512, 64, 8192], P('frq', 'src', 'rcv')
Inputs may be any that keep to these rules, and one draw needn't show every extreme that they name: band_map[i, j] is 1 exactly where |j - ((2 i + 1) * 32) // 1472| is at most a half-width drawn for source block i between 8 and 16.
All inputs are finite; a program needn't handle non-finite values.
Results may differ from a plain program's by a relative error of at most 0.004.
The roundings to bfloat16 on the way count: a program that leaves them out, or rounds other values in their place, can miss the bound.
Values may be sent and summed in bfloat16 or wider, within the bound.
No kernel may reach another device: no remote copies, remote signals or barrier semaphores. Data moves between devices by JAX's collectives and lax.ppermute only.
A program may use at most 64 MiB of HBM per device.

v0:
```python
import math

import jax
import jax.numpy as jnp
from jax import lax
from jax.sharding import PartitionSpec as P

NT = 512
FREQ = 8


def angle_table(sample_ids):
    freq_ids = jnp.arange(FREQ, dtype=jnp.int32)
    freq_bins = 1 + freq_ids * NT // (2 * FREQ)
    phase_ids = freq_bins[:, None] * sample_ids[None, :] % NT
    return phase_ids.astype(jnp.float32) * (2.0 * math.pi / NT)


def forward_table(sample_ids):
    angles = angle_table(sample_ids)
    return jnp.concatenate([jnp.cos(angles), -jnp.sin(angles)], 0) / math.sqrt(NT)


def inverse_table(sample_ids):
    angles = angle_table(sample_ids)
    return jnp.concatenate([jnp.cos(angles), -jnp.sin(angles)], 0) / math.sqrt(FREQ)


def trace_table(sample_ids):
    angles = angle_table(sample_ids)
    return jnp.concatenate([jnp.cos(angles), -jnp.sin(angles)], 0) * (2.0 / math.sqrt(NT))


def shards(f_time, reflect, band_map, gates):
    highest = lax.Precision.HIGHEST
    local_steps = f_time.shape[0]
    focal_here = f_time.shape[1]
    rcv_here = f_time.shape[2]
    freq_here = reflect.shape[1]
    src_here = reflect.shape[2]
    frq_index = lax.axis_index("frq")
    sample_ids = frq_index * local_steps + jnp.arange(local_steps, dtype=jnp.int32)
    partial_spec = jnp.dot(
        forward_table(sample_ids),
        f_time.reshape(local_steps, focal_here * rcv_here).astype(jnp.float32),
        precision=highest,
    )
    partial_spec = partial_spec.reshape(2, FREQ, focal_here, rcv_here)
    spectra = lax.psum_scatter(partial_spec, "frq", scatter_dimension=1, tiled=True).astype(
        jnp.bfloat16
    )
    rows_block = src_here // band_map.shape[0]
    cols_block = rcv_here // band_map.shape[1]
    block_mask = jnp.repeat(jnp.repeat(band_map, rows_block, 0), cols_block, 1).astype(jnp.bfloat16)
    masked = reflect * block_mask[None, None]
    spec_block = lax.all_gather(spectra, "src", axis=2, tiled=True)
    real_part = jnp.einsum(
        "ksr,kpr->ksp", masked[0], spec_block[0], preferred_element_type=jnp.float32
    )
    real_part = real_part - jnp.einsum(
        "ksr,kpr->ksp", masked[1], spec_block[1], preferred_element_type=jnp.float32
    )
    imag_part = jnp.einsum(
        "ksr,kpr->ksp", masked[0], spec_block[1], preferred_element_type=jnp.float32
    )
    imag_part = imag_part + jnp.einsum(
        "ksr,kpr->ksp", masked[1], spec_block[0], preferred_element_type=jnp.float32
    )
    forward = jnp.stack([real_part, imag_part])
    summed = lax.psum(forward, "rcv")
    all_freq = lax.all_gather(summed, "frq", axis=1, tiled=True)
    columns = all_freq.shape[3]
    all_samples = jnp.arange(NT, dtype=jnp.int32)
    forward_rows = forward_table(all_samples).reshape(2, FREQ, NT)
    own_rows = lax.dynamic_slice_in_dim(forward_rows, frq_index * freq_here, freq_here, 1)
    own_rows = own_rows.reshape(2 * freq_here, NT)
    gate_mask = (all_samples[None, :] < gates[:, None]).astype(jnp.float32)
    weights = jnp.einsum(
        "ot,pt,it->poi", own_rows, gate_mask, trace_table(all_samples), precision=highest
    )
    flattened = all_freq.reshape(2 * FREQ, src_here, columns)
    gated = jnp.einsum("poi,isp->osp", weights, flattened, precision=highest)
    windowed = gated.reshape(2, freq_here, src_here, columns).astype(jnp.bfloat16)
    real_part = jnp.einsum(
        "ksr,ksp->pkr", masked[0], windowed[0], preferred_element_type=jnp.float32
    )
    real_part = real_part + jnp.einsum(
        "ksr,ksp->pkr", masked[1], windowed[1], preferred_element_type=jnp.float32
    )
    imag_part = jnp.einsum(
        "ksr,ksp->pkr", masked[0], windowed[1], preferred_element_type=jnp.float32
    )
    imag_part = imag_part - jnp.einsum(
        "ksr,ksp->pkr", masked[1], windowed[0], preferred_element_type=jnp.float32
    )
    adjoint = lax.psum_scatter(
        jnp.stack([real_part, imag_part], 1), "src", scatter_dimension=0, tiled=True
    )
    all_adjoint = lax.all_gather(adjoint, "frq", axis=2, tiled=True)
    all_adjoint = all_adjoint.reshape(focal_here, 2 * FREQ, rcv_here)
    focused = jnp.einsum("it,pir->tpr", inverse_table(sample_ids), all_adjoint, precision=highest)
    return focused.astype(jnp.bfloat16)


def solution(mesh):
    return jax.shard_map(
        shards,
        mesh=mesh,
        in_specs=(P("frq", "src", "rcv"), P(None, "frq", "src", "rcv"), P("src", "rcv"), P()),
        out_specs=P("frq", "src", "rcv"),
        check_vma=False,
    )
```

profile of v0, /device:TPU:1, one launch (start us, length us, event | category | flops | bytes accessed | tf_op | source)
XLA Modules:
  0.0 548.5 jit_solution(5061307119029565216)
XLA Ops:
  6.6 1.5 copy.66
  8.1 0.5 copy.46
  8.7 0.9 fusion.26
  9.7 10.6 %all-reduce.9 = bf16[2,8,2,1024]{3,1,2,0:T(8,128)(2,1)S(1)} all-reduce(f32[2,8,2,1024]{3,1,2,0:T(8,128)S(1)} %fusion.26), channel_id=2, replica_groups=mesh['src'=32,'rcv'=8,'frq'=2] {'frq'}, use_global_device_ids=true, to_apply=%region_0.1.clone | all-reduce | flops 32768 | bytes 196608
  20.2 1.3 dynamic-slice
  22.2 0.6 copy.47
  23.5 2.2 broadcast_multiply_fusion
  25.7 106.2 %all-gather.2.cloned.1.call-done = bf16[2,4,64,1024]{3,1,0,2:T(4,128)(2,1)} async-done(((bf16[2,4,2,1024]{3,1,0,2:T(4,128)(2,1)}), bf16[2,4,64,1024]{3,1,0,2:T(4,128)(2,1)}) %all-gather.2.cloned.1.call-update) | async-done | bytes 1048592 | tf_op jit(solution)/shard_map/all_gather | solution.py:56
  131.9 1.6 fusion.46
  133.5 0.6 fusion.8
  134.1 0.6 fusion.9
  134.7 0.6 fusion.3
  135.4 0.6 fusion.4
  136.0 0.8 pad_maximum_fusion.1
  137.5 115.6 %all-reduce.6.cloned.1.call-done = f32[2,4,184,64]{2,3,1,0:T(8,128)} async-done(((f32[2,4,184,64]{2,3,1,0:T(8,128)}), f32[2,4,184,64]{2,3,1,0:T(8,128)}) %all-reduce.6.cloned.1.call-update) | async-done | bytes 376848 | tf_op jit(solution)/shard_map/psum | solution.py:70
  253.1 8.0 %all_gather.10 = f32[2,8,184,64]{2,3,1,0:T(8,128)S(1)} all-gather(f32[2,4,184,64]{2,3,1,0:T(8,128)} %all-reduce.6.cloned.1.call-done), channel_id=1, replica_groups=mesh['src'=32,'rcv'=8,'frq'=2] {'frq'}, dimensions={1}, use_global_device_ids=true | all-gather | bytes 1130496 | tf_op jit(solution)/shard_map/all_gather | solution.py:71
  261.1 1.3 fusion.2
  264.5 2.7 copy.56
  267.1 1.3 dynamic-slice.2
  269.1 246.0 %all-reduce.8.cloned.1.call-done = f32[64,2,4,1024]{3,2,1,0:T(4,128)} async-done(((f32[64,2,4,1024]{3,2,1,0:T(4,128)}), f32[64,2,4,1024]{3,2,1,0:T(4,128)}) %all-reduce.8.cloned.1.call-update) | async-done | bytes 2097168
  515.0 0.8 constant_dynamic-slice_fusion
  515.9 22.2 %all_gather.11 = f32[2,2,8,1024]{3,1,0,2:T(2,128)S(1)} all-gather(f32[2,2,4,1024]{3,1,0,2:T(2,128)S(1)} %copy.57), channel_id=1, replica_groups=mesh['src'=32,'rcv'=8,'frq'=2] {'frq'}, dimensions={2}, use_global_device_ids=true | all-gather | bytes 196608 | tf_op jit(solution)/shard_map/all_gather | solution.py:99
  538.1 1.8 convolution_convert_fusion
  540.0 2.0 copy.59
  (32 shorter events, 3.5 us)
Async XLA Ops:
  6.5 125.4 %all-gather.2.cloned.1.call-start = ((), (), s32[]{:S(2)}) async-start(), calls=%async_computation | async-start | bytes 1081344 | tf_op jit(solution)/shard_map/all_gather | solution.py:56
  8.1 14.8 %copy-start = (s32[23,4]{0,1:T(4,128)S(1)}, s32[23,4]{0,1:T(4,128)}, u32[]{:S(2)}) copy-start(s32[23,4]{0,1:T(4,128)} %param.6) | copy-start | bytes 1108
  22.8 230.3 %all-reduce.6.cloned.1.call-start = ((), (), s32[]{:S(2)}) async-start(), calls=%async_computation.1 | async-start | bytes 1048576 | tf_op jit(solution)/shard_map/psum | solution.py:70
  135.4 1.6 copy-start.1
  136.9 378.2 %all-reduce.8.cloned.1.call-start = ((), (), s32[]{:S(2)}) async-start(), calls=%async_computation.2 | async-start | bytes 4194304
Sparse Core Ops, SparseCore 0:
  23.0 108.8 all-gather.1
  137.0 116.0 all-reduce.5
  267.3 247.7 all-reduce.7
where the time goes:
time: 549 us
  waiting for transfers between devices  468 us (85%)
  blocking collectives  40.7 us (7%)
  between operations  14.6 us (3%)
  local copies, waits for them, and re-layouts  13.1 us (2%)
  matrix products  8.73 us (2%)
    unnamed x4, waiting for transfers between devices  246 us
    psum x1, waiting for transfers between devices, shards(): summed = lax.psum(forward, 'rcv')  116 us
    all_gather x1, waiting for transfers between devices, shards(): spec_block = lax.all_gather(spectra, 'src', axis=2, tiled=True)  106 us
    all_gather x1, blocking collectives, shards(): all_adjoint = lax.all_gather(adjoint, 'frq', axis=2, tiled=True)  22.2 us
  transfers between devices with their start and end apart: 3, of which 3 were waited for; matrix products, arithmetic and copies ran while one was open for 1% of the time, Pallas kernels for 0%

commit v1 on v0

v1 whole, which is shorter than its diff:
```python
import math

import jax
import jax.numpy as jnp
from jax import lax
from jax.sharding import Mesh, PartitionSpec as P

NT = 512
FREQ = 8
HIGHEST = lax.Precision.HIGHEST
SRC = ("zh", "zl", "xl")
RCV = ("y", "xh")
PAIR = ("zl", "xl")


def angle_table(sample_ids):
    freq_ids = jnp.arange(FREQ, dtype=jnp.int32)
    freq_bins = 1 + freq_ids * NT // (2 * FREQ)
    phase_ids = freq_bins[:, None] * sample_ids[None, :] % NT
    return phase_ids.astype(jnp.float32) * (2.0 * math.pi / NT)


def wave_table(sample_ids, scale):
    angles = angle_table(sample_ids)
    rows = jnp.stack([jnp.cos(angles), -jnp.sin(angles)]) * scale
    rows = rows.reshape(2, 2, FREQ // 2, sample_ids.shape[0])
    return rows.transpose(1, 0, 2, 3).reshape(2 * FREQ, sample_ids.shape[0])


def shards(f_time, reflect, band_map, gates):
    local_steps, focal_here, rcv_here = f_time.shape
    freq_here, src_here = reflect.shape[1], reflect.shape[2]
    rows = 2 * freq_here
    zh, zl, xl = (lax.axis_size(a) for a in SRC)
    n_src = zh * zl * xl
    n_rcv = lax.axis_size(RCV)
    focal = n_src * focal_here
    frq_index = lax.axis_index("c")
    sample_ids = frq_index * local_steps + jnp.arange(local_steps, dtype=jnp.int32)

    partial_spec = jnp.dot(
        wave_table(sample_ids, 1.0 / math.sqrt(NT)),
        f_time.reshape(local_steps, focal_here * rcv_here).astype(jnp.float32),
        precision=HIGHEST,
    ).reshape(2, rows, focal_here, rcv_here)
    halves = lax.all_to_all(partial_spec, "c", 0, 0, tiled=True)
    spectra = (halves[0] + halves[1]).astype(jnp.bfloat16)
    near = lax.all_gather(spectra, "zh", axis=0)
    near = jnp.broadcast_to(near[None], (zl * xl,) + near.shape)
    every = lax.all_to_all(near, PAIR, 0, 0, tiled=True)
    spec = every.transpose(2, 0, 1, 3, 4).reshape(2, freq_here, focal, rcv_here)

    rows_block = src_here // band_map.shape[0]
    cols_block = rcv_here // band_map.shape[1]
    block_mask = jnp.repeat(jnp.repeat(band_map, rows_block, 0), cols_block, 1).astype(jnp.bfloat16)
    masked = reflect * block_mask[None, None]

    stacked_r = jnp.concatenate([spec[0], spec[1]], 1)
    stacked_i = jnp.concatenate([-spec[1], spec[0]], 1)
    forward = jnp.einsum("kqr,ksr->kqs", stacked_r, masked[0], preferred_element_type=jnp.float32)
    forward += jnp.einsum("kqr,ksr->kqs", stacked_i, masked[1], preferred_element_type=jnp.float32)
    focal_part = focal // (2 * n_rcv)
    parts = forward.reshape(freq_here, 2, 2 * n_rcv, focal_part, src_here)
    parts = parts.transpose(2, 3, 1, 0, 4).reshape(2 * n_rcv, focal_part, rows, src_here)
    parts = lax.all_to_all(parts, RCV + ("c",), 0, 0, tiled=True)
    summed = parts.reshape(n_rcv, 2, focal_part, rows, src_here).sum(0)

    mine = (lax.axis_index(RCV) * 2 + frq_index) * focal_part
    gate_order = gates.reshape(zh, zl * xl, focal_here).transpose(1, 0, 2).reshape(focal)
    own_gates = lax.dynamic_slice_in_dim(gate_order, mine, focal_part)
    all_samples = jnp.arange(NT, dtype=jnp.int32)
    gate_mask = (all_samples[None, :] < own_gates[:, None]).astype(jnp.float32)
    weights = jnp.einsum(
        "ot,pt,it->poi",
        wave_table(all_samples, 1.0 / math.sqrt(NT)),
        gate_mask,
        wave_table(all_samples, 2.0 / math.sqrt(NT)),
        precision=HIGHEST,
    )
    weights = weights.reshape(focal_part, 2, rows, 2, rows)
    gated = jnp.einsum("pgofi,fpis->gops", weights, summed, precision=HIGHEST).astype(jnp.bfloat16)
    gated = jnp.broadcast_to(gated[None], (n_rcv,) + gated.shape)
    gated = gated.reshape(2 * n_rcv, rows, focal_part, src_here)
    gated = lax.all_to_all(gated, RCV + ("c",), 0, 0, tiled=True)
    windowed = gated.transpose(1, 0, 2, 3).reshape(2, freq_here, focal, src_here)

    stacked_r = jnp.concatenate([windowed[0], windowed[1]], 1)
    stacked_i = jnp.concatenate([windowed[1], -windowed[0]], 1)
    adjoint = jnp.einsum("kqs,ksr->kqr", stacked_r, masked[0], preferred_element_type=jnp.float32)
    adjoint += jnp.einsum("kqs,ksr->kqr", stacked_i, masked[1], preferred_element_type=jnp.float32)
    sends = adjoint.astype(jnp.bfloat16).reshape(freq_here, 2, zl * xl, zh, focal_here, rcv_here)
    sends = sends.transpose(2, 3, 4, 1, 0, 5).reshape(zl * xl, zh, focal_here, rows, rcv_here)
    got = lax.all_to_all(sends, PAIR, 0, 0, tiled=True)
    got = got.astype(jnp.float32).sum(0)
    got = lax.all_to_all(got, "zh", 0, 0, tiled=True)
    own = got.sum(0)
    both = lax.all_gather(own, "c", axis=0)
    focused = jnp.einsum(
        "fit,fpir->tpr",
        wave_table(sample_ids, 1.0 / math.sqrt(FREQ)).reshape(2, rows, local_steps),
        both,
        precision=HIGHEST,
    )
    return focused.astype(jnp.bfloat16)


def solution(mesh):
    src, rcv, frq = (mesh.shape[a] for a in ("src", "rcv", "frq"))
    fine = Mesh(
        mesh.devices.reshape(src // 4, 2, 2, rcv // 2, 2, frq), SRC + RCV + ("c",)
    )
    return jax.shard_map(
        shards,
        mesh=fine,
        in_specs=(P("c", SRC, RCV), P(None, "c", SRC, RCV), P(SRC, RCV), P()),
        out_specs=P("c", SRC, RCV),
        check_vma=False,
    )
```

time: 549 us -> 177 us (0.32)
  the two profiles are of different devices: /device:TPU:1 before, /device:TPU:41 now
where the time goes in v1:
time: 177 us; the launch traced here: 176 us
  blocking collectives  68.8 us (39%)
  waiting for transfers between devices  38.1 us (22%)
  starting transfers between devices  26.9 us (15%)
  local copies, waits for them, and re-layouts  24.4 us (14%)
  matrix products  11.9 us (7%)
  other arithmetic  5.77 us (3%)
    all_gather x1, blocking collectives, shards(): near = lax.all_gather(spectra, 'zh', axis=0)  28.9 us
    all_to_all x1, waiting for transfers between devices, shards(): got = lax.all_to_all(got, 'zh', 0, 0, tiled=True)  28 us
    all_to_all x1, blocking collectives, shards(): got = lax.all_to_all(sends, PAIR, 0, 0, tiled=True)  16.6 us
    all_to_all x1, starting transfers between devices, shards(): parts = lax.all_to_all(parts, RCV + ('c',), 0, 0, tiled=True)  14.6 us
    all_to_all x1, blocking collectives, shards(): gated = lax.all_to_all(gated, RCV + ('c',), 0, 0, tiled=True)  12.8 us
    all_to_all x1, starting transfers between devices, shards(): got = lax.all_to_all(got, 'zh', 0, 0, tiled=True)  7.29 us
    all_to_all x1, waiting for transfers between devices, shards(): parts = lax.all_to_all(parts, RCV + ('c',), 0, 0, tiled=True)  7.17 us
    all_gather x1, blocking collectives, shards(): both = lax.all_gather(own, 'c', axis=0)  6.32 us
  transfers between devices with their start and end apart: 3, of which 3 were waited for; matrix products, arithmetic and copies ran while one was open for 4% of the time, Pallas kernels for 0%

profile of v1, /device:TPU:41, one launch (start us, length us, event | category | flops | bytes accessed | tf_op | source)
XLA Modules:
  0.0 176.1 jit_solution(1452490222535742860)
XLA Ops:
  0.3 1.5 copy.109
  3.3 4.2 %all_to_all.30 = f32[2,8,2,1024]{3,1,2,0:T(8,128)S(1)} all-to-all(f32[2,8,2,1024]{3,1,2,0:T(8,128)S(1)} %fusion.30), channel_id=1, replica_groups=mesh['zh'=8,'zl'=2,'xl'=2,'y'=4,'xh'=2,'c'=2] {'c'}, dimensions={0} | all-to-all | bytes 262144 | tf_op jit(solution)/shard_map/all_to_all | solution.py:46
  7.5 28.9 %all_gather.10 = bf16[8,8,2,1024]{3,1,2,0:T(8,128)(2,1)S(1)} all-gather(bf16[1,8,2,1024]{3,1,2,0:T(8,128)(2,1)S(1)} %fusion.21), channel_id=1, replica_groups=mesh['zh'=8,'zl'=2,'xl'=2,'y'=4,'xh'=2,'c'=2] {'zh'}, dimensions={0}, use_global_device_ids=true | all-gather | bytes 294912 | tf_op jit(solution)/shard_map/all_gather | solution.py:48
  36.6 2.0 %broadcast_in_dim.8 = bf16[4,8,8,2,1024]{4,3,1,2,0:T(2,128)(2,1)} broadcast(bf16[8,8,2,1024]{3,2,0,1:T(2,128)(2,1)S(1)} %copy.75), dimensions={1,2,3,4} | broadcast | bytes 1310720 | tf_op jit(solution)/shard_map/broadcast_in_dim | solution.py:49
  38.6 5.0 %all-to-all-start.1 = ((bf16[4,8,8,2,1024]{4,3,1,2,0:T(2,128)(2,1)}), bf16[4,8,8,2,1024]{4,3,1,2,0:T(2,128)(2,1)}, u32[]{:S(2)}, u32[]{:S(2)}) async-start(bf16[4,8,8,2,1024]{4,3,1,2,0:T(2,128)(2,1)} %broadcast_in_dim.8), calls=%async_computation.1 | async-start | bytes 2097152 | tf_op jit(solution)/shard_map/all_to_all | solution.py:50
  46.6 2.2 %broadcast_multiply_fusion = bf16[2,4,184,1024]{3,2,1,0:T(8,128)(2,1)S(1)} fusion(bf16[2,4,184,1024]{3,2,1,0:T(8,128)(2,1)} %param.5, bf16[184,1024]{1,0:T(8,128)(2,1)S(1)} %bitcast.92), kind=kLoop, calls=%fused_computation.5 | loop fusion | flops 1507328 | bytes 6406144 | tf_op jit(solution)/shard_map/mul | solution.py:56
  48.7 2.9 %all-to-all-done.1 = bf16[4,8,8,2,1024]{4,3,1,2,0:T(2,128)(2,1)} async-done(((bf16[4,8,8,2,1024]{4,3,1,2,0:T(2,128)(2,1)}), bf16[4,8,8,2,1024]{4,3,1,2,0:T(2,128)(2,1)}, u32[]{:S(2)}, u32[]{:S(2)}) %all-to-all-start.1) | async-done | bytes 1048608 | tf_op jit(solution)/shard_map/all_to_all | solution.py:50
  51.6 2.9 %fusion.45 = (bf16[4,4,8,2,1024]{4,3,2,0,1:T(2,128)(2,1)S(1)}, bf16[4,4,8,2,1024]{4,3,2,0,1:T(2,128)(2,1)}) fusion(bf16[8,4,8,2,1024]{4,3,2,0,1:T(2,128)(2,1)} %bitcast.18), kind=kLoop, calls=%fused_computation.81 | loop fusion | bytes 2097152 | tf_op jit(solution)/shard_map/slice | solution.py:58
  56.0 2.2 %copy.77 = bf16[4,4,8,2,1024]{4,3,2,1,0:T(2,128)(2,1)} copy(bf16[4,4,8,2,1024]{4,3,2,0,1:T(2,128)(2,1)} %get-tuple-element.6) | data formatting | bytes 1048576 | tf_op jit(solution)/shard_map/slice | solution.py:58
  59.6 1.7 fusion.1
  61.3 1.3 fusion.3
  65.3 14.6 %all-to-all-start.2 = ((f32[16,4,8,184]{3,2,1,0:T(8,128)}), f32[16,4,8,184]{3,2,1,0:T(8,128)S(1)}, u32[]{:S(2)}, u32[]{:S(2)}) async-start(f32[16,4,8,184]{3,2,1,0:T(8,128)} %copy.81), calls=%async_computation.2 | async-start | bytes 1048576 | tf_op jit(solution)/shard_map/all_to_all | solution.py:65
  80.7 1.8 %fusion.18 = f32[4,2,8,2,8]{4,2,3,1,0:T(8,128)} fusion(f32[512,16]{0,1:T(8,128)} %bitcast.104, f32[512,4]{0,1:T(4,128)S(1)} %convert_bitcast_fusion, f32[2,8,512,1,1]{2,0,1,4,3:T(2,128)} %bitcast.103), kind=kOutput, calls=%fused_computation.25 | convolution fusion | flops 6324224 | bytes 77824 | tf_op jit(solution)/shard_map/ot,pt,it->poi/dot_general | solution.py:73
  82.5 7.2 %all-to-all-done.2 = f32[16,4,8,184]{3,2,1,0:T(8,128)S(1)} async-done(((f32[16,4,8,184]{3,2,1,0:T(8,128)}), f32[16,4,8,184]{3,2,1,0:T(8,128)S(1)}, u32[]{:S(2)}, u32[]{:S(2)}) %all-to-all-start.2) | async-done | bytes 376864 | tf_op jit(solution)/shard_map/all_to_all | solution.py:65
  92.3 12.8 %all_to_all.31 = bf16[16,8,4,184]{3,1,2,0:T(8,128)(2,1)S(1)} all-to-all(bf16[16,8,4,184]{3,1,2,0:T(8,128)(2,1)S(1)} %bitcast.100), channel_id=1, replica_groups=mesh['zh'=8,'zl'=2,'xl'=2,'y'=4,'xh'=2,'c'=2] {'y','xh','c'}, dimensions={0} | all-to-all | bytes 376832 | tf_op jit(solution)/shard_map/all_to_all | solution.py:84
  107.6 1.7 fusion
  109.4 1.5 add_convert_fusion
  110.9 1.5 reshape.309
  112.6 16.6 %all_to_all.32 = bf16[4,8,2,8,1024]{4,1,3,2,0:T(8,128)(2,1)S(1)} all-to-all(bf16[4,8,2,8,1024]{4,1,3,2,0:T(8,128)(2,1)S(1)} %bitcast.87), channel_id=1, replica_groups=mesh['zh'=8,'zl'=2,'xl'=2,'y'=4,'xh'=2,'c'=2] {'zl','xl'}, dimensions={0} | all-to-all | bytes 2097152 | tf_op jit(solution)/shard_map/all_to_all | solution.py:93
  130.5 7.3 %all-to-all-start.5 = ((f32[8,2,8,1024]{3,2,1,0:T(8,128)}), f32[8,2,8,1024]{3,2,1,0:T(8,128)S(1)}, u32[]{:S(2)}, u32[]{:S(2)}) async-start(f32[8,2,8,1024]{3,2,1,0:T(8,128)} %copy.94), calls=%async_computation.5 | async-start | bytes 1048576 | tf_op jit(solution)/shard_map/all_to_all | solution.py:95
  137.8 28.0 %all-to-all-done.5 = f32[8,2,8,1024]{3,2,1,0:T(8,128)S(1)} async-done(((f32[8,2,8,1024]{3,2,1,0:T(8,128)}), f32[8,2,8,1024]{3,2,1,0:T(8,128)S(1)}, u32[]{:S(2)}, u32[]{:S(2)}) %all-to-all-start.5) | async-done | bytes 524320 | tf_op jit(solution)/shard_map/all_to_all | solution.py:95
  165.9 6.3 %all-gather = f32[4,8,1024]{2,1,0:T(8,128)S(1)} all-gather(f32[2,8,1024]{2,1,0:T(8,128)S(1)} %reduce_sum.29), channel_id=2, replica_groups=mesh['zh'=8,'zl'=2,'xl'=2,'y'=4,'xh'=2,'c'=2] {'c'}, dimensions={0}, use_global_device_ids=true | all-gather | bytes 196608 | tf_op jit(solution)/shard_map/all_gather | solution.py:97
  172.2 1.8 %bitcast_convert_fusion = bf16[256,2,1024]{2,0,1:T(8,128)(2,1)S(1)} fusion(f32[2,2,8,1024]{3,2,1,0:T(8,128)S(1)} %bitcast.101, f32[2,8,256,1]{2,1,0,3:T(8,128)S(1)} %reshape.318), kind=kOutput, calls=%fused_computation | convolution fusion | flops 101187584 | bytes 1196032 | tf_op jit(solution)/shard_map/fit,fpir->tpr/dot_general | solution.py:98
  174.1 2.0 %copy.96 = bf16[256,2,1024]{2,1,0:T(2,128)(2,1)} copy(bf16[256,2,1024]{2,0,1:T(8,128)(2,1)S(1)} %bitcast_convert_fusion) | data formatting | bytes 2097152 | tf_op jit(solution)/shard_map/convert_element_type | solution.py:104
  (56 shorter events, 18.0 us)
Async XLA Ops:
  7.4 36.1 %copy-start.3 = (s32[23,4]{0,1:T(4,128)S(1)}, s32[23,4]{0,1:T(4,128)}, u32[]{:S(2)}) copy-start(s32[23,4]{0,1:T(4,128)} %param.6) | copy-start | bytes 1108
  7.4 36.2 %copy-start.4 = (s32[64]{0:T(128)S(1)}, s32[64]{0:T(128)}, u32[]{:S(2)}) copy-start(s32[64]{0:T(128)} %param.7) | copy-start | bytes 772
  38.6 13.0 %all-to-all-start.1 = ((bf16[4,8,8,2,1024]{4,3,1,2,0:T(2,128)(2,1)}), bf16[4,8,8,2,1024]{4,3,1,2,0:T(2,128)(2,1)}, u32[]{:S(2)}, u32[]{:S(2)}) async-start(bf16[4,8,8,2,1024]{4,3,1,2,0:T(2,128)(2,1)} %broadcast_in_dim.8), calls=%async_computation.1 | async-start | bytes 2097152 | tf_op jit(solution)/shard_map/all_to_all | solution.py:50
  59.6 1.7 copy-start.2
  65.3 24.3 %all-to-all-start.2 = ((f32[16,4,8,184]{3,2,1,0:T(8,128)}), f32[16,4,8,184]{3,2,1,0:T(8,128)S(1)}, u32[]{:S(2)}, u32[]{:S(2)}) async-start(f32[16,4,8,184]{3,2,1,0:T(8,128)} %copy.81), calls=%async_computation.2 | async-start | bytes 1048576 | tf_op jit(solution)/shard_map/all_to_all | solution.py:65
  106.8 2.6 %copy-start = (bf16[4,64,184]{2,1,0:T(8,128)(2,1)S(1)}, bf16[4,64,184]{2,1,0:T(8,128)(2,1)}, u32[]{:S(2)}) copy-start(bf16[4,64,184]{2,1,0:T(8,128)(2,1)} %copy.91) | copy-start | bytes 282628
  107.6 1.7 copy-start.1
  130.5 35.4 %all-to-all-start.5 = ((f32[8,2,8,1024]{3,2,1,0:T(8,128)}), f32[8,2,8,1024]{3,2,1,0:T(8,128)S(1)}, u32[]{:S(2)}, u32[]{:S(2)}) async-start(f32[8,2,8,1024]{3,2,1,0:T(8,128)} %copy.94), calls=%async_computation.5 | async-start | bytes 1048576 | tf_op jit(solution)/shard_map/all_to_all | solution.py:95

commit v2 on v1

v2 whole, which is shorter than its diff:
```python
import math

import jax
import jax.numpy as jnp
from jax import lax
from jax.experimental import pallas as pl
from jax.experimental.pallas import tpu as pltpu
from jax.sharding import Mesh, PartitionSpec as P

NT = 512
FREQ = 8
HALF = FREQ // 2
LANES = 128
HIGHEST = lax.Precision.HIGHEST
BF16 = jnp.bfloat16
F32 = jnp.float32
SRC = ("zh", "zl", "xl")
RCV = ("y", "xh")
PAIR = ("zl", "xl")
ROWS = 2 * HALF


def iota(shape, axis):
    return lax.broadcasted_iota(jnp.int32, shape, axis)


def wave(freq_ids, parts, sample_ids):
    phase = (1 + freq_ids * NT // (2 * FREQ)) * sample_ids % NT
    angle = phase.astype(F32) * (2.0 * math.pi / NT)
    return jnp.where(parts == 0, jnp.cos(angle), -jnp.sin(angle))


def thirds(x):
    high = lax.reduce_precision(x, 8, 7)
    middle = lax.reduce_precision(x - high, 8, 7)
    return high.astype(BF16), middle.astype(BF16), (x - high - middle).astype(BF16)


def vmem_call(body, out_shape, scratch=()):
    return pl.pallas_call(
        body,
        out_shape=out_shape,
        scratch_shapes=list(scratch),
        compiler_params=pltpu.CompilerParams(vmem_limit_bytes=32 << 20),
    )


def spectra_body(table_ref, f_ref, own_ref, other_ref):
    steps, focal, cols = f_ref.shape
    merged = f_ref[...].reshape(steps * focal, cols)
    sums = jnp.dot(table_ref[...], merged, preferred_element_type=F32)
    rows = sums.shape[0] // 3
    sums = sums[:rows] + sums[rows : 2 * rows] + sums[2 * rows :]
    own_ref[...] = sums[: rows // 2]
    other_ref[...] = sums[rows // 2 :]


def forward_body(spec_ref, resp_ref, out_ref, wide_ref, sums_ref):
    blocks = wide_ref.shape[0]
    points = spec_ref.shape[0] // ROWS
    chunks, _, lanes = out_ref.shape
    for j in range(blocks):
        wide_ref[j] = spec_ref[:, j * lanes : (j + 1) * lanes].astype(F32)

    def pick(row):
        pieces = [wide_ref[j, pl.ds(row, points, stride=ROWS), :] for j in range(blocks)]
        return jnp.concatenate(pieces, 1)

    for k in range(HALF):
        real, imag = pick(k), pick(HALF + k)
        first = jnp.concatenate([real, imag], 0).astype(BF16)
        second = jnp.concatenate([-imag, real], 0).astype(BF16)
        dims = (((1,), (1,)), ((), ()))
        sums = lax.dot_general(first, resp_ref[0, k], dims, preferred_element_type=F32)
        sums += lax.dot_general(second, resp_ref[1, k], dims, preferred_element_type=F32)
        head = sums[:, :lanes]
        rest = sums[:, lanes:]
        tail = jnp.concatenate(
            [rest, jnp.zeros((rest.shape[0], lanes - rest.shape[1]), F32)], 1
        )
        for part in range(2):
            at = pl.ds(part * HALF + k, points, stride=ROWS)
            sums_ref[0, at, :] = head[part * points : (part + 1) * points]
            sums_ref[1, at, :] = tail[part * points : (part + 1) * points]
    rows = points * ROWS // chunks
    for d in range(chunks):
        out_ref[d, :rows] = sums_ref[0, d * rows : (d + 1) * rows]
        tail = sums_ref[1, d * rows : (d + 1) * rows]
        out_ref[d, rows:] = tail[: rows // 2] + pltpu.roll(tail[rows // 2 :], lanes // 2, 1)


def gate_body(matrix_ref, parts_ref, out_ref):
    chunks, packed, lanes = parts_ref.shape
    rows = packed * 2 // 3
    cores = []
    for f in range(2):
        total = parts_ref[f]
        for d in range(f + 2, chunks, 2):
            total += parts_ref[d]
        tail = total[rows:]
        tail = jnp.concatenate([tail[:, : lanes // 2], tail[:, lanes // 2 :]], 0)
        cores.append(jnp.concatenate([total[:rows], tail], 1))
    gated = jnp.dot(
        matrix_ref[...], jnp.concatenate(cores, 0), precision=HIGHEST, preferred_element_type=F32
    ).astype(BF16)
    for f in range(2):
        mine = gated[f * rows : (f + 1) * rows]
        tail = mine[:, lanes:]
        tail = jnp.concatenate([tail[: rows // 2], tail[rows // 2 :]], 1)
        mine = jnp.concatenate([mine[:, :lanes], tail], 0)
        for d in range(f, chunks, 2):
            out_ref[d] = mine


def adjoint_body(win_ref, resp_ref, out_ref, wide_ref, sums_ref):
    chunks, packed, lanes = win_ref.shape
    rows = packed * 2 // 3
    points = chunks * rows // ROWS
    sources = resp_ref.shape[2]
    blocks = sums_ref.shape[0]
    for d in range(chunks):
        wide_ref[0, d * rows : (d + 1) * rows] = win_ref[d, :rows].astype(F32)
        tail = win_ref[d, rows:].astype(F32)
        half = d * rows + rows // 2
        wide_ref[1, d * rows : half] = tail
        wide_ref[1, half : (d + 1) * rows] = pltpu.roll(tail, lanes // 2, 1)

    def pick(row):
        pieces = [wide_ref[j, pl.ds(row, points, stride=ROWS), :] for j in range(2)]
        return jnp.concatenate(pieces, 1)[:, :sources]

    for k in range(HALF):
        real, imag = pick(k), pick(HALF + k)
        first = jnp.concatenate([real, imag], 0).astype(BF16)
        second = jnp.concatenate([imag, -real], 0).astype(BF16)
        sums = jnp.dot(first, resp_ref[0, k], preferred_element_type=F32)
        sums += jnp.dot(second, resp_ref[1, k], preferred_element_type=F32)
        for part in range(2):
            at = pl.ds(part * HALF + k, points, stride=ROWS)
            for j in range(blocks):
                sums_ref[j, at, :] = sums[
                    part * points : (part + 1) * points, j * lanes : (j + 1) * lanes
                ]
    for j in range(blocks):
        out_ref[:, j * lanes : (j + 1) * lanes] = sums_ref[j].astype(BF16)


def focused_body(table_ref, sums_ref, out_ref):
    steps, focal, cols = out_ref.shape
    x = sums_ref[...]
    high = x.astype(BF16)
    rest = x - high.astype(F32)
    middle = rest.astype(BF16)
    low = (rest - middle.astype(F32)).astype(BF16)
    right = jnp.concatenate([high, middle, high, low, high, middle], 0)
    values = jnp.dot(table_ref[...], right, preferred_element_type=F32)
    out_ref[...] = values.astype(BF16).reshape(steps, focal, cols)


def shards(f_time, reflect, band_map, gates):
    steps, focal_here, cols = f_time.shape
    sources = reflect.shape[2]
    zh, zl, xl = (lax.axis_size(a) for a in SRC)
    pairs = zl * xl
    n_rcv = lax.axis_size(RCV)
    chunks = 2 * n_rcv
    focal = zh * pairs * focal_here
    core = lax.axis_index("c")
    own_rows = focal_here * ROWS
    struct = jax.ShapeDtypeStruct

    shape = (2 * own_rows, steps * focal_here)
    row, col = iota(shape, 0), iota(shape, 1)
    held = jnp.where(row < own_rows, core, 1 - core)
    table = wave(held * HALF + row % HALF, row // HALF % 2, core * steps + col // focal_here)
    table = jnp.where(row // ROWS % focal_here == col % focal_here, table / math.sqrt(NT), 0.0)
    own, other = vmem_call(
        spectra_body, [struct((own_rows, cols), F32), struct((own_rows, cols), F32)]
    )(jnp.concatenate(thirds(table), 0), f_time)
    other = lax.ppermute(other, "c", [(0, 1), (1, 0)])
    spectra = (own + other).astype(BF16)
    near = jnp.broadcast_to(spectra[None], (zh, own_rows, cols))
    near = lax.all_to_all(near, "zh", 0, 0, tiled=True).reshape(zh * own_rows, cols)
    every = jnp.broadcast_to(near[None], (pairs, zh * own_rows, cols))
    every = lax.all_to_all(every, PAIR, 0, 0, tiled=True).reshape(focal * ROWS, cols)

    rows_block = sources // band_map.shape[0]
    cols_block = cols // band_map.shape[1]
    block_mask = jnp.repeat(jnp.repeat(band_map, rows_block, 0), cols_block, 1).astype(BF16)
    masked = reflect * block_mask[None, None]

    part_rows = focal * ROWS // chunks
    packed = part_rows * 3 // 2
    parts = vmem_call(
        forward_body,
        struct((chunks, packed, LANES), F32),
        [
            pltpu.VMEM((cols // LANES, focal * ROWS, LANES), F32),
            pltpu.VMEM((2, focal * ROWS, LANES), F32),
        ],
    )(every, masked)
    parts = lax.all_to_all(parts, RCV + ("c",), 0, 0, tiled=True)

    part_focal = part_rows // ROWS
    shape = (2 * part_rows, NT)
    row, col = iota(shape, 0), iota(shape, 1)
    waves = wave(row // part_rows * HALF + row % HALF, row // HALF % 2, col)
    point = (lax.axis_index(RCV) * 2 + core) * part_focal + iota((2 * part_rows, focal), 0) // ROWS % part_focal
    block = point // focal_here
    point = (block % zh * pairs + block // zh) * focal_here + point % focal_here
    window = jnp.where(point == iota((2 * part_rows, focal), 1), gates[None, :], 0).sum(1)
    inner = jnp.where(col < window[:, None], waves / math.sqrt(NT), 0.0)
    matrix = lax.dot_general(
        inner, waves * (2.0 / math.sqrt(NT)), (((1,), (1,)), ((), ())), precision=HIGHEST
    )
    shape = matrix.shape
    same = iota(shape, 0) // ROWS % part_focal == iota(shape, 1) // ROWS % part_focal
    matrix = jnp.where(same, matrix, 0.0)
    gated = vmem_call(gate_body, struct((chunks, packed, LANES), BF16))(matrix, parts)
    windowed = lax.all_to_all(gated, RCV + ("c",), 0, 0, tiled=True)

    sends = vmem_call(
        adjoint_body,
        struct((focal * ROWS, cols), BF16),
        [
            pltpu.VMEM((2, focal * ROWS, LANES), F32),
            pltpu.VMEM((cols // LANES, focal * ROWS, LANES), F32),
        ],
    )(windowed, masked)
    got = lax.all_to_all(sends.reshape(pairs, zh * own_rows, cols), PAIR, 0, 0, tiled=True)
    got = got.astype(F32).sum(0).astype(BF16).reshape(zh, own_rows, cols)
    got = lax.all_to_all(got, "zh", 0, 0, tiled=True)
    got = got.astype(F32).sum(0)
    both = lax.all_gather(got, "c", axis=0, tiled=True)

    shape = (steps * focal_here, 2 * own_rows)
    row, col = iota(shape, 0), iota(shape, 1)
    table = wave(col // own_rows * HALF + col % HALF, col // HALF % 2, core * steps + row // focal_here)
    table = jnp.where(col // ROWS % focal_here == row % focal_here, table / math.sqrt(FREQ), 0.0)
    high, middle, low = thirds(table)
    table = jnp.concatenate([high, high, middle, high, low, middle], 1)
    return vmem_call(focused_body, struct((steps, focal_here, cols), BF16))(table, both)


def solution(mesh):
    src, rcv, frq = (mesh.shape[a] for a in ("src", "rcv", "frq"))
    devices = mesh.devices.reshape(src // 4, 2, 2, rcv // 2, 2, frq)
    return jax.shard_map(
        shards,
        mesh=Mesh(devices, SRC + RCV + ("c",)),
        in_specs=(P("c", SRC, RCV), P(None, "c", SRC, RCV), P(SRC, RCV), P()),
        out_specs=P("c", SRC, RCV),
        check_vma=False,
    )
```

time: 177 us -> 141 us (0.80)
  the two profiles are of different devices: /device:TPU:41 before, /device:TPU:1 now
where the time goes in v2:
time: 141 us; the launch traced here: 140 us
  blocking collectives  61.3 us (43%)
  waiting for transfers between devices  31 us (22%)
  starting transfers between devices  29.6 us (21%)
  other arithmetic  6.27 us (4%)
  Pallas kernels  5.97 us (4%)
  local copies, waits for them, and re-layouts  3.8 us (3%)
  matrix products  2.25 us (2%)
    all_to_all x1, blocking collectives, shards(): lax.all_to_all(near, 'zh', 0, 0, tiled=True).reshape(zh * own_rows, cols)  27.5 us
    all_to_all x1, waiting for transfers between devices, shards(): got = lax.all_to_all(got, 'zh', 0, 0, tiled=True)  15.4 us
    all_to_all x1, blocking collectives, shards(): lax.all_to_all(sends.reshape(pairs, zh * own_rows, cols), PAIR, 0, 0, til...  15.3 us
    all_to_all x1, blocking collectives, shards(): windowed = lax.all_to_all(gated, RCV + ('c',), 0, 0, tiled=True)  11.8 us
    all_to_all x1, starting transfers between devices, shards(): parts = lax.all_to_all(parts, RCV + ('c',), 0, 0, tiled=True)  11 us
    ppermute x1, starting transfers between devices, shards(): other = lax.ppermute(other, 'c', [(0, 1), (1, 0)])  8.79 us
    all_to_all x1, waiting for transfers between devices, shards(): lax.all_to_all(every, PAIR, 0, 0, tiled=True).reshape(focal * ROWS, cols)  7.9 us
    all_to_all x1, waiting for transfers between devices, shards(): parts = lax.all_to_all(parts, RCV + ('c',), 0, 0, tiled=True)  6.85 us
  transfers between devices with their start and end apart: 4, of which 4 were waited for; matrix products, arithmetic and copies ran while one was open for 6% of the time, Pallas kernels for 0%

profile of v2, /device:TPU:1, one launch (start us, length us, event | category | flops | bytes accessed | tf_op | source)
XLA Modules:
  0.0 140.4 jit_solution(17934933813273555659)
XLA Ops:
  0.1 0.4 reduce-precision_convert_fusion.3
  0.5 1.2 copy-done.1
  2.1 8.8 %collective-permute-start = (f32[16,1024]{1,0:T(8,128)S(1)}, f32[16,1024]{1,0:T(8,128)S(1)}, u32[]{:S(2)}, u32[]{:S(2)}) collective-permute-start(f32[16,1024]{1,0:T(8,128)S(1)} %get-tuple-element.8), channel_id=1, source_target_pairs={{0,1},{1,0},{2,3},{3,2},{4,5},{5,4},{6,7},{7,6},{8,9},{9,8},{10,11... | collective-permute-start | bytes 196616 | tf_op jit(solution)/shard_map/ppermute | solution.py:180
  10.9 0.9 collective-permute-done
  11.8 27.5 %all_to_all.30 = bf16[8,16,1024]{2,1,0:T(8,128)(2,1)S(1)} all-to-all(bf16[8,16,1024]{2,1,0:T(8,128)(2,1)S(1)} %broadcast_in_dim.63), channel_id=1, replica_groups=mesh['zh'=8,'zl'=2,'xl'=2,'y'=4,'xh'=2,'c'=2] {'zh'}, dimensions={0} | all-to-all | bytes 524288 | tf_op jit(solution)/shard_map/all_to_all | solution.py:183
  39.3 1.1 broadcast_in_dim.65
  40.4 4.2 %all-to-all-start.1 = ((bf16[4,128,1024]{2,1,0:T(8,128)(2,1)}), bf16[4,128,1024]{2,1,0:T(8,128)(2,1)}, u32[]{:S(2)}, u32[]{:S(2)}) async-start(bf16[4,128,1024]{2,1,0:T(8,128)(2,1)} %broadcast_in_dim.65), calls=%async_computation.1 | async-start | bytes 2097152 | tf_op jit(solution)/shard_map/all_to_all | solution.py:185
  45.1 2.2 %broadcast_multiply_fusion.resp_ref = bf16[2,4,184,1024]{3,2,1,0:T(8,128)(2,1)S(1)} fusion(bf16[2,4,184,1024]{3,2,1,0:T(8,128)(2,1)} %param.5, bf16[184,1024]{1,0:T(8,128)(2,1)S(1)} %bitcast.9), kind=kLoop, calls=%fused_computation | loop fusion | flops 1507328 | bytes 6406144 | tf_op jit(solution)/shard_map/mul | solution.py:190
  47.4 7.9 %all-to-all-done.1 = bf16[4,128,1024]{2,1,0:T(8,128)(2,1)} async-done(((bf16[4,128,1024]{2,1,0:T(8,128)(2,1)}), bf16[4,128,1024]{2,1,0:T(8,128)(2,1)}, u32[]{:S(2)}, u32[]{:S(2)}) %all-to-all-start.1) | async-done | bytes 1048608 | tf_op jit(solution)/shard_map/all_to_all | solution.py:185
  55.3 2.7 %shard_map.47 = f32[16,48,128]{2,1,0:T(8,128)S(1)} custom-call(bf16[512,1024]{1,0:T(8,128)(2,1)} %bitcast.1.spec_ref, bf16[2,4,184,1024]{3,2,1,0:T(8,128)(2,1)S(1)} %broadcast_multiply_fusion.resp_ref), custom_call_target="tpu_custom_call" | custom-call | tf_op jit(solution)/shard_map/pallas_call | solution.py:194
  58.0 0.7 copy-done
  58.7 11.0 %all-to-all-start.2 = ((f32[16,48,128]{2,1,0:T(8,128)}), f32[16,48,128]{2,1,0:T(8,128)S(1)}, u32[]{:S(2)}, u32[]{:S(2)}) async-start(f32[16,48,128]{2,1,0:T(8,128)} %copy-done), calls=%async_computation.2 | async-start | bytes 786432 | tf_op jit(solution)/shard_map/all_to_all | solution.py:202
  69.7 0.5 broadcast_add_fusion.2
  70.5 2.3 %convolution_select_fusion.matrix_ref = f32[64,64]{1,0:T(8,128)S(1)} fusion(s32[64]{0:T(128)S(1)} %get-tuple-element.41, s32[64]{0:T(128)S(1)} %get-tuple-element.42, s32[64]{0:T(128)S(1)} %get-tuple-element.39, s32[64]{0:T(128)} %get-tuple-element.43, s32[64]{0:T(128)S(1)} %get-tuple-element.40, s32[64]{0:T(128)} %get-tuple-element.44, ...), kind=kOutput, calls=%fused_computation.1 | convolution fusion | flops 28680192 | bytes 18944 | tf_op jit(solution)/shard_map/dot_general | solution.py:213
  72.8 6.8 %all-to-all-done.2.parts_ref = f32[16,48,128]{2,1,0:T(8,128)S(1)} async-done(((f32[16,48,128]{2,1,0:T(8,128)}), f32[16,48,128]{2,1,0:T(8,128)S(1)}, u32[]{:S(2)}, u32[]{:S(2)}) %all-to-all-start.2) | async-done | bytes 393248 | tf_op jit(solution)/shard_map/all_to_all | solution.py:202
  80.0 11.8 %all_to_all.31.win_ref = bf16[16,48,128]{2,1,0:T(8,128)(2,1)S(1)} all-to-all(bf16[16,48,128]{2,1,0:T(8,128)(2,1)S(1)} %shard_map.48), channel_id=1, replica_groups=mesh['zh'=8,'zl'=2,'xl'=2,'y'=4,'xh'=2,'c'=2] {'y','xh','c'}, dimensions={0} | all-to-all | bytes 393216 | tf_op jit(solution)/shard_map/all_to_all | solution.py:220
  91.8 1.2 shard_map.49
  93.0 15.3 %all_to_all.32 = bf16[4,128,1024]{2,1,0:T(8,128)(2,1)S(1)} all-to-all(bf16[4,128,1024]{2,1,0:T(8,128)(2,1)S(1)} %bitcast.8), channel_id=1, replica_groups=mesh['zh'=8,'zl'=2,'xl'=2,'y'=4,'xh'=2,'c'=2] {'zl','xl'}, dimensions={0} | all-to-all | bytes 2097152 | tf_op jit(solution)/shard_map/all_to_all | solution.py:230
  108.3 0.9 reduce_sum.31
  109.2 5.6 %all-to-all-start.5 = ((bf16[8,16,1024]{2,1,0:T(8,128)(2,1)}), bf16[8,16,1024]{2,1,0:T(8,128)(2,1)S(1)}, u32[]{:S(2)}, u32[]{:S(2)}) async-start(bf16[8,16,1024]{2,1,0:T(8,128)(2,1)} %bitcast.4), calls=%async_computation.5 | async-start | bytes 524288 | tf_op jit(solution)/shard_map/all_to_all | solution.py:232
  114.8 1.8 %fusion = (bf16[512,32]{1,0:T(8,128)(2,1)S(1)}, bf16[512,32]{1,0:T(8,128)(2,1)S(1)}, bf16[512,32]{1,0:T(8,128)(2,1)S(1)}) fusion(s32[512]{0:T(512)S(1)} %get-tuple-element.15, s32[512]{0:T(512)S(1)} %get-tuple-element.18, pred[512]{0:T(512)(128)(4,1)S(1)} %get-tuple-element.20, s32[]{:T(128)S(6)} %mul.104, s32[32]{0:T(128)S(1)} %get-tuple-element.28, ...), kind=kLoop, calls=%fused_computation.24 | loop fusion | flops 1228800 | bytes 108676 | tf_op jit(solution)/shard_map/convert_element_type | solution.py:36
  116.9 15.4 %all-to-all-done.5 = bf16[8,16,1024]{2,1,0:T(8,128)(2,1)S(1)} async-done(((bf16[8,16,1024]{2,1,0:T(8,128)(2,1)}), bf16[8,16,1024]{2,1,0:T(8,128)(2,1)S(1)}, u32[]{:S(2)}, u32[]{:S(2)}) %all-to-all-start.5) | async-done | bytes 262176 | tf_op jit(solution)/shard_map/all_to_all | solution.py:232
  132.3 6.7 %all_gather.3.sums_ref = f32[32,1024]{1,0:T(8,128)S(1)} all-gather(f32[16,1024]{1,0:T(8,128)S(1)} %convert_reduce_fusion), channel_id=1, replica_groups=mesh['zh'=8,'zl'=2,'xl'=2,'y'=4,'xh'=2,'c'=2] {'c'}, dimensions={0}, use_global_device_ids=true | all-gather | bytes 196608 | tf_op jit(solution)/shard_map/all_gather | solution.py:234
  139.0 1.4 %shard_map.50 = bf16[256,2,1024]{2,1,0:T(2,128)(2,1)} custom-call(bf16[512,192]{1,0:T(8,128)(2,1)S(1)} %concatenate.6.table_ref, f32[32,1024]{1,0:T(8,128)S(1)} %all_gather.3.sums_ref), custom_call_target="tpu_custom_call" | custom-call | tf_op jit(solution)/shard_map/pallas_call | solution.py:242
  (34 shorter events, 1.8 us)
Async XLA Ops:
  0.0 44.6 %copy-start.2 = (s32[23,4]{0,1:T(4,128)S(1)}, s32[23,4]{0,1:T(4,128)}, u32[]{:S(2)}) copy-start(s32[23,4]{0,1:T(4,128)} %param.6) | copy-start | bytes 1108
  0.5 1.2 copy-start.1
  2.1 9.7 %collective-permute-start = (f32[16,1024]{1,0:T(8,128)S(1)}, f32[16,1024]{1,0:T(8,128)S(1)}, u32[]{:S(2)}, u32[]{:S(2)}) collective-permute-start(f32[16,1024]{1,0:T(8,128)S(1)} %get-tuple-element.8), channel_id=1, source_target_pairs={{0,1},{1,0},{2,3},{3,2},{4,5},{5,4},{6,7},{7,6},{8,9},{9,8},{10,11... | collective-permute-start | bytes 196616 | tf_op jit(solution)/shard_map/ppermute | solution.py:180
  40.4 14.9 %all-to-all-start.1 = ((bf16[4,128,1024]{2,1,0:T(8,128)(2,1)}), bf16[4,128,1024]{2,1,0:T(8,128)(2,1)}, u32[]{:S(2)}, u32[]{:S(2)}) async-start(bf16[4,128,1024]{2,1,0:T(8,128)(2,1)} %broadcast_in_dim.65), calls=%async_computation.1 | async-start | bytes 2097152 | tf_op jit(solution)/shard_map/all_to_all | solution.py:185
  47.4 22.9 %copy-start.3 = (s32[64]{0:T(128)S(1)}, s32[64]{0:T(128)}, u32[]{:S(2)}) copy-start(s32[64]{0:T(128)} %param.7) | copy-start | bytes 772
  58.0 0.7 copy-start
  58.7 20.9 %all-to-all-start.2 = ((f32[16,48,128]{2,1,0:T(8,128)}), f32[16,48,128]{2,1,0:T(8,128)S(1)}, u32[]{:S(2)}, u32[]{:S(2)}) async-start(f32[16,48,128]{2,1,0:T(8,128)} %copy-done), calls=%async_computation.2 | async-start | bytes 786432 | tf_op jit(solution)/shard_map/all_to_all | solution.py:202
  109.2 23.0 %all-to-all-start.5 = ((bf16[8,16,1024]{2,1,0:T(8,128)(2,1)}), bf16[8,16,1024]{2,1,0:T(8,128)(2,1)S(1)}, u32[]{:S(2)}, u32[]{:S(2)}) async-start(bf16[8,16,1024]{2,1,0:T(8,128)(2,1)} %bitcast.4), calls=%async_computation.5 | async-start | bytes 524288 | tf_op jit(solution)/shard_map/all_to_all | solution.py:232

commit v3 on v2

--- a/solution.py
+++ b/solution.py
@@ -25,9 +25,8 @@
 
 
 def wave(freq_ids, parts, sample_ids):
-    phase = (1 + freq_ids * NT // (2 * FREQ)) * sample_ids % NT
-    angle = phase.astype(F32) * (2.0 * math.pi / NT)
-    return jnp.where(parts == 0, jnp.cos(angle), -jnp.sin(angle))
+    phase = ((1 + freq_ids * NT // (2 * FREQ)) * sample_ids + parts * (NT // 4)) % NT
+    return jnp.cos(phase.astype(F32) * (2.0 * math.pi / NT))
 
 
 def thirds(x):
@@ -41,7 +40,7 @@
         body,
         out_shape=out_shape,
         scratch_shapes=list(scratch),
-        compiler_params=pltpu.CompilerParams(vmem_limit_bytes=32 << 20),
+        compiler_params=pltpu.CompilerParams(vmem_limit_bytes=12 << 20),
     )
 
 
@@ -145,6 +144,13 @@
         out_ref[:, j * lanes : (j + 1) * lanes] = sums_ref[j].astype(BF16)
 
 
+def sum_body(got_ref, out_ref):
+    total = got_ref[0].astype(F32)
+    for d in range(1, got_ref.shape[0]):
+        total += got_ref[d].astype(F32)
+    out_ref[...] = total.astype(out_ref.dtype)
+
+
 def focused_body(table_ref, sums_ref, out_ref):
     steps, focal, cols = out_ref.shape
     x = sums_ref[...]
@@ -153,8 +159,17 @@
     middle = rest.astype(BF16)
     low = (rest - middle.astype(F32)).astype(BF16)
     right = jnp.concatenate([high, middle, high, low, high, middle], 0)
-    values = jnp.dot(table_ref[...], right, preferred_element_type=F32)
+    dims = (((0,), (0,)), ((), ()))
+    values = lax.dot_general(table_ref[...], right, dims, preferred_element_type=F32)
     out_ref[...] = values.astype(BF16).reshape(steps, focal, cols)
+
+
+def focal_table(core_ids, core, steps, focal, scale):
+    shape = (2 * focal * ROWS, steps * focal)
+    row, col = iota(shape, 0), iota(shape, 1)
+    held = jnp.where(row < focal * ROWS, core_ids[0], core_ids[1])
+    table = wave(held * HALF + row % HALF, row // HALF % 2, core * steps + col // focal)
+    return thirds(jnp.where(row // ROWS % focal == col % focal, table * scale, 0.0))
 
 
 def shards(f_time, reflect, band_map, gates):
@@ -169,14 +184,10 @@
     own_rows = focal_here * ROWS
     struct = jax.ShapeDtypeStruct
 
-    shape = (2 * own_rows, steps * focal_here)
-    row, col = iota(shape, 0), iota(shape, 1)
-    held = jnp.where(row < own_rows, core, 1 - core)
-    table = wave(held * HALF + row % HALF, row // HALF % 2, core * steps + col // focal_here)
-    table = jnp.where(row // ROWS % focal_here == col % focal_here, table / math.sqrt(NT), 0.0)
+    table = focal_table((core, 1 - core), core, steps, focal_here, 1.0 / math.sqrt(NT))
     own, other = vmem_call(
         spectra_body, [struct((own_rows, cols), F32), struct((own_rows, cols), F32)]
-    )(jnp.concatenate(thirds(table), 0), f_time)
+    )(jnp.concatenate(table, 0), f_time)
     other = lax.ppermute(other, "c", [(0, 1), (1, 0)])
     spectra = (own + other).astype(BF16)
     near = jnp.broadcast_to(spectra[None], (zh, own_rows, cols))
@@ -190,17 +201,6 @@
     masked = reflect * block_mask[None, None]
 
     part_rows = focal * ROWS // chunks
-    packed = part_rows * 3 // 2
-    parts = vmem_call(
-        forward_body,
-        struct((chunks, packed, LANES), F32),
-        [
-            pltpu.VMEM((cols // LANES, focal * ROWS, LANES), F32),
-            pltpu.VMEM((2, focal * ROWS, LANES), F32),
-        ],
-    )(every, masked)
-    parts = lax.all_to_all(parts, RCV + ("c",), 0, 0, tiled=True)
-
     part_focal = part_rows // ROWS
     shape = (2 * part_rows, NT)
     row, col = iota(shape, 0), iota(shape, 1)
@@ -216,6 +216,21 @@
     shape = matrix.shape
     same = iota(shape, 0) // ROWS % part_focal == iota(shape, 1) // ROWS % part_focal
     matrix = jnp.where(same, matrix, 0.0)
+    high, middle, low = focal_table((0, 1), core, steps, focal_here, 1.0 / math.sqrt(FREQ))
+    table = jnp.concatenate([high, high, middle, high, low, middle], 0)
+    every, masked, matrix, table = lax.optimization_barrier((every, masked, matrix, table))
+
+    packed = part_rows * 3 // 2
+    parts = vmem_call(
+        forward_body,
+        struct((chunks, packed, LANES), F32),
+        [
+            pltpu.VMEM((cols // LANES, focal * ROWS, LANES), F32),
+            pltpu.VMEM((2, focal * ROWS, LANES), F32),
+        ],
+    )(every, masked)
+    parts = lax.all_to_all(parts, RCV + ("c",), 0, 0, tiled=True)
+
     gated = vmem_call(gate_body, struct((chunks, packed, LANES), BF16))(matrix, parts)
     windowed = lax.all_to_all(gated, RCV + ("c",), 0, 0, tiled=True)
 
@@ -228,18 +243,23 @@
         ],
     )(windowed, masked)
     got = lax.all_to_all(sends.reshape(pairs, zh * own_rows, cols), PAIR, 0, 0, tiled=True)
-    got = got.astype(F32).sum(0).astype(BF16).reshape(zh, own_rows, cols)
-    got = lax.all_to_all(got, "zh", 0, 0, tiled=True)
-    got = got.astype(F32).sum(0)
+    got = vmem_call(sum_body, struct((zh * own_rows, cols), BF16))(got)
+    got = lax.all_to_all(got.reshape(zh, own_rows, cols), "zh", 0, 0, tiled=True)
+    got = vmem_call(sum_body, struct((own_rows, cols), F32))(got)
     both = lax.all_gather(got, "c", axis=0, tiled=True)
 
-    shape = (steps * focal_here, 2 * own_rows)
-    row, col = iota(shape, 0), iota(shape, 1)
-    table = wave(col // own_rows * HALF + col % HALF, col // HALF % 2, core * steps + row // focal_here)
-    table = jnp.where(col // ROWS % focal_here == row % focal_here, table / math.sqrt(FREQ), 0.0)
-    high, middle, low = thirds(table)
-    table = jnp.concatenate([high, high, middle, high, low, middle], 1)
-    return vmem_call(focused_body, struct((steps, focal_here, cols), BF16))(table, both)
+    block = steps // 4
+    return pl.pallas_call(
+        focused_body,
+        out_shape=struct((steps, focal_here, cols), BF16),
+        grid=(4,),
+        in_specs=[
+            pl.BlockSpec((table.shape[0], block * focal_here), lambda i: (0, i)),
+            pl.BlockSpec((2 * own_rows, cols), lambda i: (0, 0)),
+        ],
+        out_specs=pl.BlockSpec((block, focal_here, cols), lambda i: (i, 0, 0)),
+        compiler_params=pltpu.CompilerParams(vmem_limit_bytes=12 << 20),
+    )(table, both)
 
 
 def solution(mesh):

time: 141 us -> 140 us (level)
  blocking collectives: 61.3 us -> 105 us
  waiting for transfers between devices: 31 us -> 4 us
  starting transfers between devices: 29.6 us -> 13.2 us
    all_to_all x0 -> x2, blocking collectives: none -> 43.6 us  [the longest x1 22.9 us: shards(): lax.all_to_all(got.reshape(zh, own_rows, cols), 'zh', 0, 0, tiled=True)]
    all_to_all x2 -> x0, waiting for transfers between devices: 22.2 us -> none  [the longest x1 15.4 us: shards(): got = lax.all_to_all(got, 'zh', 0, 0, tiled=True)]
    all_to_all x2 -> x0, starting transfers between devices: 16.6 us -> none  [the longest x1 11 us: shards(): parts = lax.all_to_all(parts, RCV + ('c',), 0, 0, tiled=True)]
    all_to_all x1, waiting for transfers between devices: 7.9 us -> 3.12 us  [shards(): lax.all_to_all(every, PAIR, 0, 0, tiled=True).reshape(focal * ROWS, cols)]
    unnamed x0 -> x5, other arithmetic: none -> 1.86 us
    convert_element_type x1 -> x0, other arithmetic: 1.8 us -> none  [thirds(): (x - high - middle).astype(BF16)]
  transfers between devices with their start and end apart: 4 -> 2, of which waited for: 4 -> 2; matrix products, arithmetic and copies ran while one was open for 6% -> 5% of each run, Pallas kernels for 0% -> 0%
where the time goes in v3:
time: 140 us; the launch traced here: 139 us
  blocking collectives  105 us (75%)
  starting transfers between devices  13.2 us (9%)
  Pallas kernels  6.94 us (5%)
  other arithmetic  5.2 us (4%)
  waiting for transfers between devices  4 us (3%)
  local copies, waits for them, and re-layouts  3.55 us (3%)
  matrix products  1.44 us (1%)
    all_to_all x1, blocking collectives, shards(): lax.all_to_all(near, 'zh', 0, 0, tiled=True).reshape(zh * own_rows, cols)  27.5 us
    all_to_all x1, blocking collectives, shards(): lax.all_to_all(got.reshape(zh, own_rows, cols), 'zh', 0, 0, tiled=True)  22.9 us
    all_to_all x1, blocking collectives, shards(): parts = lax.all_to_all(parts, RCV + ('c',), 0, 0, tiled=True)  20.7 us
    all_to_all x1, blocking collectives, shards(): lax.all_to_all(sends.reshape(pairs, zh * own_rows, cols), PAIR, 0, 0, til...  15.3 us
    all_to_all x1, blocking collectives, shards(): windowed = lax.all_to_all(gated, RCV + ('c',), 0, 0, tiled=True)  11.8 us
    ppermute x1, starting transfers between devices, shards(): other = lax.ppermute(other, 'c', [(0, 1), (1, 0)])  8.93 us
    all_gather x1, blocking collectives, shards(): both = lax.all_gather(got, 'c', axis=0, tiled=True)  6.68 us
    all_to_all x1, starting transfers between devices, shards(): lax.all_to_all(every, PAIR, 0, 0, tiled=True).reshape(focal * ROWS, cols)  4.23 us
  transfers between devices with their start and end apart: 2, of which 2 were waited for; matrix products, arithmetic and copies ran while one was open for 5% of the time, Pallas kernels for 0%

profile of v3, /device:TPU:1, one launch (start us, length us, event | category | flops | bytes accessed | tf_op | source)
XLA Modules:
  0.0 139.4 jit_solution(15589955803443620669)
XLA Ops:
  0.1 0.4 reduce-precision_convert_fusion.3
  0.5 1.2 copy-done
  2.0 8.9 %collective-permute-start = (f32[16,1024]{1,0:T(8,128)S(1)}, f32[16,1024]{1,0:T(8,128)S(1)}, u32[]{:S(2)}, u32[]{:S(2)}) collective-permute-start(f32[16,1024]{1,0:T(8,128)S(1)} %get-tuple-element.12), channel_id=1, source_target_pairs={{0,1},{1,0},{2,3},{3,2},{4,5},{5,4},{6,7},{7,6},{8,9},{9,8},{10,11... | collective-permute-start | bytes 196616 | tf_op jit(solution)/shard_map/ppermute | solution.py:191
  11.0 0.9 collective-permute-done
  11.9 27.5 %all_to_all.30 = bf16[8,16,1024]{2,1,0:T(8,128)(2,1)S(1)} all-to-all(bf16[8,16,1024]{2,1,0:T(8,128)(2,1)S(1)} %broadcast_in_dim.60), channel_id=1, replica_groups=mesh['zh'=8,'zl'=2,'xl'=2,'y'=4,'xh'=2,'c'=2] {'zh'}, dimensions={0} | all-to-all | bytes 524288 | tf_op jit(solution)/shard_map/all_to_all | solution.py:194
  39.4 1.1 broadcast_in_dim.62
  40.5 4.2 %all-to-all-start.1 = ((bf16[4,128,1024]{2,1,0:T(8,128)(2,1)}), bf16[4,128,1024]{2,1,0:T(8,128)(2,1)}, u32[]{:S(2)}, u32[]{:S(2)}) async-start(bf16[4,128,1024]{2,1,0:T(8,128)(2,1)} %broadcast_in_dim.62), calls=%async_computation.1 | async-start | bytes 2097152 | tf_op jit(solution)/shard_map/all_to_all | solution.py:196
  45.1 0.8 copy.6
  46.3 0.4 constant_dynamic-update-slice_fusion.4
  46.7 0.4 constant_dynamic-update-slice_fusion.3
  47.1 0.4 constant_dynamic-update-slice_fusion.2
  47.8 0.4 fusion.93
  48.2 0.4 constant_dynamic-update-slice_fusion.table_ref
  48.6 1.4 %convolution_select_fusion.matrix_ref = f32[64,64]{1,0:T(8,128)S(1)} fusion(s32[64]{0:T(128)S(1)} %get-tuple-element.40, s32[64]{0:T(128)S(1)} %get-tuple-element.44, s32[64]{0:T(128)S(1)} %get-tuple-element.41, s32[64]{0:T(128)S(1)} %get-tuple-element.43, s32[64]{0:T(128)S(1)} %get-tuple-element.42, s32[64]{0:T(128)S(1)} %get-tuple-element.45, ...), kind=kOutput, calls=%fused_computation.1 | convolution fusion | flops 28614656 | bytes 18944 | tf_op jit(solution)/shard_map/dot_general | solution.py:213
  50.0 2.2 %broadcast_multiply_fusion.resp_ref = bf16[2,4,184,1024]{3,2,1,0:T(8,128)(2,1)S(1)} fusion(bf16[2,4,184,1024]{3,2,1,0:T(8,128)(2,1)} %param.5, bf16[184,1024]{1,0:T(8,128)(2,1)S(1)} %bitcast.10), kind=kLoop, calls=%fused_computation | loop fusion | flops 1507328 | bytes 6406144 | tf_op jit(solution)/shard_map/mul | solution.py:201
  52.2 3.1 %all-to-all-done.1 = bf16[4,128,1024]{2,1,0:T(8,128)(2,1)} async-done(((bf16[4,128,1024]{2,1,0:T(8,128)(2,1)}), bf16[4,128,1024]{2,1,0:T(8,128)(2,1)}, u32[]{:S(2)}, u32[]{:S(2)}) %all-to-all-start.1) | async-done | bytes 1048608 | tf_op jit(solution)/shard_map/all_to_all | solution.py:196
  55.4 2.7 %shard_map.47 = f32[16,48,128]{2,1,0:T(8,128)S(1)} custom-call(bf16[512,1024]{1,0:T(8,128)(2,1)} %bitcast.1.spec_ref, bf16[2,4,184,1024]{3,2,1,0:T(8,128)(2,1)S(1)} %broadcast_multiply_fusion.resp_ref), custom_call_target="tpu_custom_call" | custom-call | tf_op jit(solution)/shard_map/pallas_call | solution.py:224
  58.1 20.7 %all_to_all.31.parts_ref = f32[16,48,128]{2,1,0:T(8,128)S(1)} all-to-all(f32[16,48,128]{2,1,0:T(8,128)S(1)} %shard_map.47), channel_id=1, replica_groups=mesh['zh'=8,'zl'=2,'xl'=2,'y'=4,'xh'=2,'c'=2] {'y','xh','c'}, dimensions={0} | all-to-all | bytes 786432 | tf_op jit(solution)/shard_map/all_to_all | solution.py:232
  79.1 11.8 %all_to_all.32.win_ref = bf16[16,48,128]{2,1,0:T(8,128)(2,1)S(1)} all-to-all(bf16[16,48,128]{2,1,0:T(8,128)(2,1)S(1)} %shard_map.48), channel_id=1, replica_groups=mesh['zh'=8,'zl'=2,'xl'=2,'y'=4,'xh'=2,'c'=2] {'y','xh','c'}, dimensions={0} | all-to-all | bytes 393216 | tf_op jit(solution)/shard_map/all_to_all | solution.py:235
  90.9 1.2 shard_map.49
  92.1 15.3 %all_to_all.33.got_ref = bf16[4,128,1024]{2,1,0:T(8,128)(2,1)S(1)} all-to-all(bf16[4,128,1024]{2,1,0:T(8,128)(2,1)S(1)} %bitcast.8), channel_id=1, replica_groups=mesh['zh'=8,'zl'=2,'xl'=2,'y'=4,'xh'=2,'c'=2] {'zl','xl'}, dimensions={0} | all-to-all | bytes 2097152 | tf_op jit(solution)/shard_map/all_to_all | solution.py:245
  107.5 22.9 %all_to_all.34.got_ref = bf16[8,16,1024]{2,1,0:T(8,128)(2,1)S(1)} all-to-all(bf16[8,16,1024]{2,1,0:T(8,128)(2,1)S(1)} %bitcast.9), channel_id=1, replica_groups=mesh['zh'=8,'zl'=2,'xl'=2,'y'=4,'xh'=2,'c'=2] {'zh'}, dimensions={0} | all-to-all | bytes 524288 | tf_op jit(solution)/shard_map/all_to_all | solution.py:247
  130.4 6.7 %all_gather.3.sums_ref = f32[32,1024]{1,0:T(8,128)S(1)} all-gather(f32[16,1024]{1,0:T(8,128)S(1)} %shard_map.51), channel_id=1, replica_groups=mesh['zh'=8,'zl'=2,'xl'=2,'y'=4,'xh'=2,'c'=2] {'c'}, dimensions={0}, use_global_device_ids=true | all-gather | bytes 196608 | tf_op jit(solution)/shard_map/all_gather | solution.py:249
  137.1 2.2 %shard_map.52 = bf16[256,2,1024]{2,1,0:T(2,128)(2,1)} custom-call(bf16[192,512]{1,0:T(8,128)(2,1)S(1)} %constant_dynamic-update-slice_fusion.table_ref, f32[32,1024]{1,0:T(8,128)S(1)} %all_gather.3.sums_ref), custom_call_target="tpu_custom_call" | custom-call | tf_op jit(solution)/shard_map/pallas_call | solution.py:252
  (36 shorter events, 2.0 us)
Async XLA Ops:
  0.0 44.7 %copy-start.2 = (s32[23,4]{0,1:T(4,128)S(1)}, s32[23,4]{0,1:T(4,128)}, u32[]{:S(2)}) copy-start(s32[23,4]{0,1:T(4,128)} %param.6) | copy-start | bytes 1108
  0.5 1.2 copy-start
  2.0 44.0 %copy-start.3 = (s32[64]{0:T(128)S(1)}, s32[64]{0:T(128)}, u32[]{:S(2)}) copy-start(s32[64]{0:T(128)} %param.7) | copy-start | bytes 772
  2.0 9.8 %collective-permute-start = (f32[16,1024]{1,0:T(8,128)S(1)}, f32[16,1024]{1,0:T(8,128)S(1)}, u32[]{:S(2)}, u32[]{:S(2)}) collective-permute-start(f32[16,1024]{1,0:T(8,128)S(1)} %get-tuple-element.12), channel_id=1, source_target_pairs={{0,1},{1,0},{2,3},{3,2},{4,5},{5,4},{6,7},{7,6},{8,9},{9,8},{10,11... | collective-permute-start | bytes 196616 | tf_op jit(solution)/shard_map/ppermute | solution.py:191
  40.5 14.9 %all-to-all-start.1 = ((bf16[4,128,1024]{2,1,0:T(8,128)(2,1)}), bf16[4,128,1024]{2,1,0:T(8,128)(2,1)}, u32[]{:S(2)}, u32[]{:S(2)}) async-start(bf16[4,128,1024]{2,1,0:T(8,128)(2,1)} %broadcast_in_dim.62), calls=%async_computation.1 | async-start | bytes 2097152 | tf_op jit(solution)/shard_map/all_to_all | solution.py:196
  46.0 4.1 %copy-start.1 = (bf16[23,8,4,256]{3,1,2,0:T(8,128)(2,1)S(1)}, bf16[23,8,4,256]{3,1,2,0:T(8,128)(2,1)}, u32[]{:S(2)}) copy-start(bf16[23,8,4,256]{3,1,2,0:T(8,128)(2,1)} %copy.6) | copy-start | bytes 1130500

commit v4 on v3

--- a/solution.py
+++ b/solution.py
@@ -30,9 +30,10 @@
 
 
 def thirds(x):
-    high = lax.reduce_precision(x, 8, 7)
-    middle = lax.reduce_precision(x - high, 8, 7)
-    return high.astype(BF16), middle.astype(BF16), (x - high - middle).astype(BF16)
+    high = x.astype(BF16)
+    rest = x - high.astype(F32)
+    middle = rest.astype(BF16)
+    return high, middle, (rest - middle.astype(F32)).astype(BF16)
 
 
 def vmem_call(body, out_shape, scratch=()):
@@ -44,11 +45,19 @@
     )
 
 
-def spectra_body(table_ref, f_ref, own_ref, other_ref):
+def spectra_body(f_ref, own_ref, other_ref, last_ref, held_ref, sem_ref):
+    copy = pltpu.make_async_copy(f_ref, held_ref, sem_ref)
+    copy.start()
     steps, focal, cols = f_ref.shape
-    merged = f_ref[...].reshape(steps * focal, cols)
-    sums = jnp.dot(table_ref[...], merged, preferred_element_type=F32)
-    rows = sums.shape[0] // 3
+    core = lax.axis_index("c")
+    table = focal_table((core, 1 - core), core, steps, focal, 1.0 / math.sqrt(NT))
+    rows = table.shape[0]
+    table = jnp.concatenate(thirds(table), 0)
+    high, middle, low = thirds(focal_table((0, 1), core, steps, focal, 1.0 / math.sqrt(FREQ)))
+    last_ref[...] = jnp.concatenate([high, high, middle, high, low, middle], 0)
+    copy.wait()
+    merged = held_ref[...].reshape(steps * focal, cols)
+    sums = jnp.dot(table, merged, preferred_element_type=F32)
     sums = sums[:rows] + sums[rows : 2 * rows] + sums[2 * rows :]
     own_ref[...] = sums[: rows // 2]
     other_ref[...] = sums[rows // 2 :]
@@ -151,17 +160,23 @@
     out_ref[...] = total.astype(out_ref.dtype)
 
 
-def focused_body(table_ref, sums_ref, out_ref):
+def focused_body(table_ref, sums_ref, out_ref, held_ref, sem_ref):
     steps, focal, cols = out_ref.shape
-    x = sums_ref[...]
-    high = x.astype(BF16)
-    rest = x - high.astype(F32)
-    middle = rest.astype(BF16)
-    low = (rest - middle.astype(F32)).astype(BF16)
+    high, middle, low = thirds(sums_ref[...])
     right = jnp.concatenate([high, middle, high, low, high, middle], 0)
     dims = (((0,), (0,)), ((), ()))
-    values = lax.dot_general(table_ref[...], right, dims, preferred_element_type=F32)
-    out_ref[...] = values.astype(BF16).reshape(steps, focal, cols)
+    pieces = sem_ref.shape[0]
+    block = steps // pieces
+    copies = []
+    for i in range(pieces):
+        left = table_ref[:, i * block * focal : (i + 1) * block * focal]
+        values = lax.dot_general(left, right, dims, preferred_element_type=F32)
+        at = pl.ds(i * block, block)
+        held_ref[at] = values.astype(BF16).reshape(block, focal, cols)
+        copies.append(pltpu.make_async_copy(held_ref.at[at], out_ref.at[at], sem_ref.at[i]))
+        copies[-1].start()
+    for copy in copies:
+        copy.wait()
 
 
 def focal_table(core_ids, core, steps, focal, scale):
@@ -169,7 +184,7 @@
     row, col = iota(shape, 0), iota(shape, 1)
     held = jnp.where(row < focal * ROWS, core_ids[0], core_ids[1])
     table = wave(held * HALF + row % HALF, row // HALF % 2, core * steps + col // focal)
-    return thirds(jnp.where(row // ROWS % focal == col % focal, table * scale, 0.0))
+    return jnp.where(row // ROWS % focal == col % focal, table * scale, 0.0)
 
 
 def shards(f_time, reflect, band_map, gates):
@@ -184,16 +199,19 @@
     own_rows = focal_here * ROWS
     struct = jax.ShapeDtypeStruct
 
-    table = focal_table((core, 1 - core), core, steps, focal_here, 1.0 / math.sqrt(NT))
-    own, other = vmem_call(
-        spectra_body, [struct((own_rows, cols), F32), struct((own_rows, cols), F32)]
-    )(jnp.concatenate(table, 0), f_time)
+    own, other, table = pl.pallas_call(
+        spectra_body,
+        out_shape=[struct((own_rows, cols), F32)] * 2
+        + [struct((6 * 2 * own_rows, steps * focal_here), BF16)],
+        in_specs=[pl.BlockSpec(memory_space=pltpu.HBM)],
+        scratch_shapes=[pltpu.VMEM(f_time.shape, BF16), pltpu.SemaphoreType.DMA],
+        compiler_params=pltpu.CompilerParams(vmem_limit_bytes=54784 << 10),
+    )(f_time)
     other = lax.ppermute(other, "c", [(0, 1), (1, 0)])
+    other, core, gates, band_map = lax.optimization_barrier((other, core, gates, band_map))
     spectra = (own + other).astype(BF16)
     near = jnp.broadcast_to(spectra[None], (zh, own_rows, cols))
     near = lax.all_to_all(near, "zh", 0, 0, tiled=True).reshape(zh * own_rows, cols)
-    every = jnp.broadcast_to(near[None], (pairs, zh * own_rows, cols))
-    every = lax.all_to_all(every, PAIR, 0, 0, tiled=True).reshape(focal * ROWS, cols)
 
     rows_block = sources // band_map.shape[0]
     cols_block = cols // band_map.shape[1]
@@ -216,9 +234,9 @@
     shape = matrix.shape
     same = iota(shape, 0) // ROWS % part_focal == iota(shape, 1) // ROWS % part_focal
     matrix = jnp.where(same, matrix, 0.0)
-    high, middle, low = focal_table((0, 1), core, steps, focal_here, 1.0 / math.sqrt(FREQ))
-    table = jnp.concatenate([high, high, middle, high, low, middle], 0)
-    every, masked, matrix, table = lax.optimization_barrier((every, masked, matrix, table))
+    near, masked, matrix = lax.optimization_barrier((near, masked, matrix))
+    every = jnp.broadcast_to(near[None], (pairs, zh * own_rows, cols))
+    every = lax.all_to_all(every, PAIR, 0, 0, tiled=True).reshape(focal * ROWS, cols)
 
     packed = part_rows * 3 // 2
     parts = vmem_call(
@@ -248,16 +266,12 @@
     got = vmem_call(sum_body, struct((own_rows, cols), F32))(got)
     both = lax.all_gather(got, "c", axis=0, tiled=True)
 
-    block = steps // 4
     return pl.pallas_call(
         focused_body,
         out_shape=struct((steps, focal_here, cols), BF16),
-        grid=(4,),
-        in_specs=[
-            pl.BlockSpec((table.shape[0], block * focal_here), lambda i: (0, i)),
-            pl.BlockSpec((2 * own_rows, cols), lambda i: (0, 0)),
-        ],
-        out_specs=pl.BlockSpec((block, focal_here, cols), lambda i: (i, 0, 0)),
+        in_specs=[pl.BlockSpec(memory_space=pltpu.VMEM)] * 2,
+        out_specs=pl.BlockSpec(memory_space=pltpu.HBM),
+        scratch_shapes=[pltpu.VMEM(f_time.shape, BF16), pltpu.SemaphoreType.DMA((2,))],
         compiler_params=pltpu.CompilerParams(vmem_limit_bytes=12 << 20),
     )(table, both)
 

time: 140 us -> 137 us (0.979)
  blocking collectives: 105 us -> 91.6 us
  waiting for transfers between devices: 4 us -> 14 us
  starting transfers between devices: 13.2 us -> 18.2 us
  other arithmetic: 5.2 us -> 3.19 us
  local copies, waits for them, and re-layouts: 3.55 us -> 2.02 us
    all_to_all x1, blocking collectives: 27.5 us -> 11.8 us  [shards(): lax.all_to_all(every, PAIR, 0, 0, tiled=True).reshape(focal * ROWS, cols)]
    all_to_all x1, waiting for transfers between devices: 3.12 us -> 13.2 us  [shards(): lax.all_to_all(near, 'zh', 0, 0, tiled=True).reshape(zh * own_rows, cols)]
    all_to_all x1, starting transfers between devices: 4.23 us -> 9.44 us  [shards(): lax.all_to_all(near, 'zh', 0, 0, tiled=True).reshape(zh * own_rows, cols)]
    unnamed x5 -> x0, other arithmetic: 1.86 us -> none
    all_to_all x1, blocking collectives: 20.7 us -> 22.3 us  [shards(): parts = lax.all_to_all(parts, RCV + ('c',), 0, 0, tiled=True)]
  transfers between devices with their start and end apart: 2 -> 2, of which waited for: 2 -> 2; matrix products, arithmetic and copies ran while one was open for 5% -> 4% of each run, Pallas kernels for 0% -> 0%
where the time goes in v4:
time: 137 us
  blocking collectives  91.6 us (67%)
  starting transfers between devices  18.2 us (13%)
  waiting for transfers between devices  14 us (10%)
  Pallas kernels  6.05 us (4%)
  other arithmetic  3.19 us (2%)
  local copies, waits for them, and re-layouts  2.02 us (1%)
  matrix products  1.44 us (1%)
    all_to_all x1, blocking collectives, shards(): lax.all_to_all(got.reshape(zh, own_rows, cols), 'zh', 0, 0, tiled=True)  23.4 us
    all_to_all x1, blocking collectives, shards(): parts = lax.all_to_all(parts, RCV + ('c',), 0, 0, tiled=True)  22.3 us
    all_to_all x1, blocking collectives, shards(): lax.all_to_all(sends.reshape(pairs, zh * own_rows, cols), PAIR, 0, 0, til...  15.3 us
    all_to_all x1, waiting for transfers between devices, shards(): lax.all_to_all(near, 'zh', 0, 0, tiled=True).reshape(zh * own_rows, cols)  13.2 us
    all_to_all x1, blocking collectives, shards(): lax.all_to_all(every, PAIR, 0, 0, tiled=True).reshape(focal * ROWS, cols)  11.8 us
    all_to_all x1, blocking collectives, shards(): windowed = lax.all_to_all(gated, RCV + ('c',), 0, 0, tiled=True)  11.8 us
    all_to_all x1, starting transfers between devices, shards(): lax.all_to_all(near, 'zh', 0, 0, tiled=True).reshape(zh * own_rows, cols)  9.44 us
    ppermute x1, starting transfers between devices, shards(): other = lax.ppermute(other, 'c', [(0, 1), (1, 0)])  8.79 us
  transfers between devices with their start and end apart: 2, of which 2 were waited for; matrix products, arithmetic and copies ran while one was open for 4% of the time, Pallas kernels for 0%

profile of v4, /device:TPU:1, one launch (start us, length us, event | category | flops | bytes accessed | tf_op | source)
XLA Modules:
  0.0 136.7 jit_solution(7791014532808874324)
XLA Ops:
  0.0 1.6 %shard_map.46 = (f32[16,1024]{1,0:T(8,128)S(1)}, f32[16,1024]{1,0:T(8,128)S(1)}, bf16[192,512]{1,0:T(8,128)(2,1)S(1)}) custom-call(bf16[256,2,1024]{2,1,0:T(2,128)(2,1)} %f_ref.1), custom_call_target="tpu_custom_call" | custom-call | tf_op jit(solution)/shard_map/pallas_call | solution.py:202
  1.6 8.8 %collective-permute-start = (f32[16,1024]{1,0:T(8,128)S(1)}, f32[16,1024]{1,0:T(8,128)S(1)}, u32[]{:S(2)}, u32[]{:S(2)}) collective-permute-start(f32[16,1024]{1,0:T(8,128)S(1)} %get-tuple-element.17), channel_id=1, source_target_pairs={{0,1},{1,0},{2,3},{3,2},{4,5},{5,4},{6,7},{7,6},{8,9},{9,8},{10,11... | collective-permute-start | bytes 196616 | tf_op jit(solution)/shard_map/ppermute | solution.py:210
  10.5 0.8 collective-permute-done
  11.3 0.7 convert_element_type.24
  12.1 0.7 broadcast_in_dim.39
  12.8 9.4 %all-to-all-start = ((bf16[8,16,1024]{2,1,0:T(8,128)(2,1)}), bf16[8,16,1024]{2,1,0:T(8,128)(2,1)S(1)}, u32[]{:S(2)}, u32[]{:S(2)}) async-start(bf16[8,16,1024]{2,1,0:T(8,128)(2,1)} %broadcast_in_dim.39), calls=%async_computation | async-start | bytes 524288 | tf_op jit(solution)/shard_map/all_to_all | solution.py:214
  22.3 0.3 broadcast_in_dim.41
  22.5 0.8 copy.6
  23.3 0.3 select_reduce_fusion
  23.6 1.4 %convolution_select_fusion.matrix_ref = f32[64,64]{1,0:T(8,128)S(1)} fusion(s32[64]{0:T(128)S(1)} %get-tuple-element.31, s32[64]{0:T(128)S(1)} %get-tuple-element.35, s32[64]{0:T(128)S(1)} %get-tuple-element.32, s32[64]{0:T(128)S(1)} %get-tuple-element.34, s32[64]{0:T(128)S(1)} %get-tuple-element.33, s32[64]{0:T(128)S(1)} %get-tuple-element.36, ...), kind=kOutput, calls=%fused_computation.1 | convolution fusion | flops 28614656 | bytes 18944 | tf_op jit(solution)/shard_map/dot_general | solution.py:231
  25.0 2.2 %broadcast_multiply_fusion.resp_ref = bf16[2,4,184,1024]{3,2,1,0:T(8,128)(2,1)S(1)} fusion(bf16[2,4,184,1024]{3,2,1,0:T(8,128)(2,1)} %param.5, bf16[184,1024]{1,0:T(8,128)(2,1)S(1)} %bitcast.11), kind=kLoop, calls=%fused_computation | loop fusion | flops 1507328 | bytes 6406144 | tf_op jit(solution)/shard_map/mul | solution.py:219
  27.3 13.2 %all-to-all-done = bf16[8,16,1024]{2,1,0:T(8,128)(2,1)S(1)} async-done(((bf16[8,16,1024]{2,1,0:T(8,128)(2,1)}), bf16[8,16,1024]{2,1,0:T(8,128)(2,1)S(1)}, u32[]{:S(2)}, u32[]{:S(2)}) %all-to-all-start) | async-done | bytes 262176 | tf_op jit(solution)/shard_map/all_to_all | solution.py:214
  40.5 0.1 broadcast_in_dim.45
  40.6 11.8 %all_to_all.30 = bf16[4,128,1024]{2,1,0:T(8,128)(2,1)S(1)} all-to-all(bf16[4,128,1024]{2,1,0:T(8,128)(2,1)S(1)} %broadcast_in_dim.45), channel_id=1, replica_groups=mesh['zh'=8,'zl'=2,'xl'=2,'y'=4,'xh'=2,'c'=2] {'zl','xl'}, dimensions={0} | all-to-all | bytes 2097152 | tf_op jit(solution)/shard_map/all_to_all | solution.py:239
  52.4 1.5 %shard_map.47 = f32[16,48,128]{2,1,0:T(8,128)S(1)} custom-call(bf16[512,1024]{1,0:T(8,128)(2,1)S(1)} %bitcast.8, bf16[2,4,184,1024]{3,2,1,0:T(8,128)(2,1)S(1)} %broadcast_multiply_fusion.resp_ref), custom_call_target="tpu_custom_call" | custom-call | tf_op jit(solution)/shard_map/pallas_call | solution.py:242
  53.9 22.3 %all_to_all.31.parts_ref = f32[16,48,128]{2,1,0:T(8,128)S(1)} all-to-all(f32[16,48,128]{2,1,0:T(8,128)S(1)} %shard_map.47), channel_id=1, replica_groups=mesh['zh'=8,'zl'=2,'xl'=2,'y'=4,'xh'=2,'c'=2] {'y','xh','c'}, dimensions={0} | all-to-all | bytes 786432 | tf_op jit(solution)/shard_map/all_to_all | solution.py:250
  76.2 0.3 shard_map.48
  76.5 11.8 %all_to_all.32.win_ref = bf16[16,48,128]{2,1,0:T(8,128)(2,1)S(1)} all-to-all(bf16[16,48,128]{2,1,0:T(8,128)(2,1)S(1)} %shard_map.48), channel_id=1, replica_groups=mesh['zh'=8,'zl'=2,'xl'=2,'y'=4,'xh'=2,'c'=2] {'y','xh','c'}, dimensions={0} | all-to-all | bytes 393216 | tf_op jit(solution)/shard_map/all_to_all | solution.py:253
  88.3 1.2 shard_map.49
  89.5 15.3 %all_to_all.33.got_ref = bf16[4,128,1024]{2,1,0:T(8,128)(2,1)S(1)} all-to-all(bf16[4,128,1024]{2,1,0:T(8,128)(2,1)S(1)} %bitcast.9), channel_id=1, replica_groups=mesh['zh'=8,'zl'=2,'xl'=2,'y'=4,'xh'=2,'c'=2] {'zl','xl'}, dimensions={0} | all-to-all | bytes 2097152 | tf_op jit(solution)/shard_map/all_to_all | solution.py:263
  104.8 0.1 shard_map.50
  104.9 23.4 %all_to_all.34.got_ref = bf16[8,16,1024]{2,1,0:T(8,128)(2,1)S(1)} all-to-all(bf16[8,16,1024]{2,1,0:T(8,128)(2,1)S(1)} %bitcast.10), channel_id=1, replica_groups=mesh['zh'=8,'zl'=2,'xl'=2,'y'=4,'xh'=2,'c'=2] {'zh'}, dimensions={0} | all-to-all | bytes 524288 | tf_op jit(solution)/shard_map/all_to_all | solution.py:265
  128.3 7.0 %all_gather.3.sums_ref = f32[32,1024]{1,0:T(8,128)S(1)} all-gather(f32[16,1024]{1,0:T(8,128)S(1)} %shard_map.51), channel_id=1, replica_groups=mesh['zh'=8,'zl'=2,'xl'=2,'y'=4,'xh'=2,'c'=2] {'c'}, dimensions={0}, use_global_device_ids=true | all-gather | bytes 196608 | tf_op jit(solution)/shard_map/all_gather | solution.py:267
  135.3 1.3 shard_map.52
  (14 shorter events, 0.2 us)
Async XLA Ops:
  0.0 23.3 %copy-start.1 = (s32[64]{0:T(128)S(1)}, s32[64]{0:T(128)}, u32[]{:S(2)}) copy-start(s32[64]{0:T(128)} %param.7) | copy-start | bytes 772
  1.6 9.7 %collective-permute-start = (f32[16,1024]{1,0:T(8,128)S(1)}, f32[16,1024]{1,0:T(8,128)S(1)}, u32[]{:S(2)}, u32[]{:S(2)}) collective-permute-start(f32[16,1024]{1,0:T(8,128)S(1)} %get-tuple-element.17), channel_id=1, source_target_pairs={{0,1},{1,0},{2,3},{3,2},{4,5},{5,4},{6,7},{7,6},{8,9},{9,8},{10,11... | collective-permute-start | bytes 196616 | tf_op jit(solution)/shard_map/ppermute | solution.py:210
  12.8 27.7 %all-to-all-start = ((bf16[8,16,1024]{2,1,0:T(8,128)(2,1)}), bf16[8,16,1024]{2,1,0:T(8,128)(2,1)S(1)}, u32[]{:S(2)}, u32[]{:S(2)}) async-start(bf16[8,16,1024]{2,1,0:T(8,128)(2,1)} %broadcast_in_dim.39), calls=%async_computation | async-start | bytes 524288 | tf_op jit(solution)/shard_map/all_to_all | solution.py:214
  23.3 1.7 %copy-start = (bf16[23,8,4,256]{3,1,2,0:T(8,128)(2,1)S(1)}, bf16[23,8,4,256]{3,1,2,0:T(8,128)(2,1)}, u32[]{:S(2)}) copy-start(bf16[23,8,4,256]{3,1,2,0:T(8,128)(2,1)} %copy.6) | copy-start | bytes 1130500

commit v5 on v4

--- a/solution.py
+++ b/solution.py
@@ -36,11 +36,12 @@
     return high, middle, (rest - middle.astype(F32)).astype(BF16)
 
 
-def vmem_call(body, out_shape, scratch=()):
+def vmem_call(body, out_shape, scratch=(), cost=None):
     return pl.pallas_call(
         body,
         out_shape=out_shape,
         scratch_shapes=list(scratch),
+        cost_estimate=cost,
         compiler_params=pltpu.CompilerParams(vmem_limit_bytes=12 << 20),
     )
 
@@ -61,6 +62,21 @@
     sums = sums[:rows] + sums[rows : 2 * rows] + sums[2 * rows :]
     own_ref[...] = sums[: rows // 2]
     other_ref[...] = sums[rows // 2 :]
+
+
+def masked_body(band_ref, resp_ref, out_ref):
+    band = band_ref[...].astype(F32).astype(BF16)
+    down, across = band.shape
+    parts, _, sources, cols = resp_ref.shape
+    shape = (across, cols)
+    picks = (iota(shape, 0) == iota(shape, 1) // (cols // across)).astype(F32).astype(BF16)
+    wide = jnp.dot(band, picks, preferred_element_type=F32).astype(BF16)
+    shape = (sources, down)
+    picks = (iota(shape, 0) // (sources // down) == iota(shape, 1)).astype(F32).astype(BF16)
+    mask = jnp.dot(picks, wide, preferred_element_type=F32).astype(BF16)
+    for c in range(parts):
+        for k in range(HALF):
+            out_ref[c, k] = resp_ref[c, k] * mask
 
 
 def forward_body(spec_ref, resp_ref, out_ref, wide_ref, sums_ref):
@@ -207,16 +223,18 @@
         scratch_shapes=[pltpu.VMEM(f_time.shape, BF16), pltpu.SemaphoreType.DMA],
         compiler_params=pltpu.CompilerParams(vmem_limit_bytes=54784 << 10),
     )(f_time)
-    other = lax.ppermute(other, "c", [(0, 1), (1, 0)])
-    other, core, gates, band_map = lax.optimization_barrier((other, core, gates, band_map))
+    others = lax.all_gather(other, "c", axis=0)
+    others, core, gates, band_map = lax.optimization_barrier((others, core, gates, band_map))
+    other = jnp.where(core == 0, others[1], others[0])
     spectra = (own + other).astype(BF16)
     near = jnp.broadcast_to(spectra[None], (zh, own_rows, cols))
     near = lax.all_to_all(near, "zh", 0, 0, tiled=True).reshape(zh * own_rows, cols)
 
-    rows_block = sources // band_map.shape[0]
-    cols_block = cols // band_map.shape[1]
-    block_mask = jnp.repeat(jnp.repeat(band_map, rows_block, 0), cols_block, 1).astype(BF16)
-    masked = reflect * block_mask[None, None]
+    masked = vmem_call(
+        masked_body,
+        struct(reflect.shape, BF16),
+        cost=pl.CostEstimate(flops=reflect.size, transcendentals=0, bytes_accessed=4 * reflect.size),
+    )(band_map, reflect)
 
     part_rows = focal * ROWS // chunks
     part_focal = part_rows // ROWS

time: 137 us -> 135 us (0.985)
  starting transfers between devices: 18.2 us -> 9.44 us
  blocking collectives: 91.6 us -> 100 us
  other arithmetic: 3.19 us -> 0.3 us
  local copies, waits for them, and re-layouts: 2.02 us -> 3.5 us
    ppermute x1 -> x0, starting transfers between devices: 8.79 us -> none  [shards(): other = lax.ppermute(other, 'c', [(0, 1), (1, 0)])]
    all_gather x0 -> x1, blocking collectives: none -> 8.42 us  [shards(): others = lax.all_gather(other, 'c', axis=0)]
    mul x1 -> x0, other arithmetic: 2.21 us -> none  [shards(): masked = reflect * block_mask[None, None]]
  transfers between devices with their start and end apart: 2 -> 1, of which waited for: 2 -> 1; matrix products, arithmetic and copies ran while one was open for 4% -> 2% of each run, Pallas kernels for 0% -> 0%
where the time goes in v5:
time: 135 us
  blocking collectives  100 us (74%)
  waiting for transfers between devices  13.2 us (10%)
  starting transfers between devices  9.44 us (7%)
  Pallas kernels  6.59 us (5%)
  local copies, waits for them, and re-layouts  3.5 us (3%)
  matrix products  1.44 us (1%)
    all_to_all x1, blocking collectives, shards(): lax.all_to_all(got.reshape(zh, own_rows, cols), 'zh', 0, 0, tiled=True)  23.4 us
    all_to_all x1, blocking collectives, shards(): parts = lax.all_to_all(parts, RCV + ('c',), 0, 0, tiled=True)  22.3 us
    all_to_all x1, blocking collectives, shards(): lax.all_to_all(sends.reshape(pairs, zh * own_rows, cols), PAIR, 0, 0, til...  15.3 us
    all_to_all x1, waiting for transfers between devices, shards(): lax.all_to_all(near, 'zh', 0, 0, tiled=True).reshape(zh * own_rows, cols)  13.2 us
    all_to_all x1, blocking collectives, shards(): lax.all_to_all(every, PAIR, 0, 0, tiled=True).reshape(focal * ROWS, cols)  11.8 us
    all_to_all x1, blocking collectives, shards(): windowed = lax.all_to_all(gated, RCV + ('c',), 0, 0, tiled=True)  11.8 us
    all_to_all x1, starting transfers between devices, shards(): lax.all_to_all(near, 'zh', 0, 0, tiled=True).reshape(zh * own_rows, cols)  9.44 us
    all_gather x1, blocking collectives, shards(): others = lax.all_gather(other, 'c', axis=0)  8.42 us
  transfers between devices with their start and end apart: 1, of which 1 were waited for; matrix products, arithmetic and copies ran while one was open for 2% of the time, Pallas kernels for 0%

profile of v5, /device:TPU:1, one launch (start us, length us, event | category | flops | bytes accessed | tf_op | source)
XLA Modules:
  0.0 134.6 jit_solution(1288026244260869792)
XLA Ops:
  0.0 1.6 %shard_map.46 = (f32[16,1024]{1,0:T(8,128)S(1)}, f32[16,1024]{1,0:T(8,128)S(1)}, bf16[192,512]{1,0:T(8,128)(2,1)S(1)}) custom-call(bf16[256,2,1024]{2,1,0:T(2,128)(2,1)} %f_ref.1), custom_call_target="tpu_custom_call" | custom-call | tf_op jit(solution)/shard_map/pallas_call | solution.py:218
  1.6 8.4 %all-gather = f32[32,1024]{1,0:T(8,128)S(1)} all-gather(f32[16,1024]{1,0:T(8,128)S(1)} %get-tuple-element.17), channel_id=2, replica_groups=mesh['zh'=8,'zl'=2,'xl'=2,'y'=4,'xh'=2,'c'=2] {'c'}, dimensions={0}, use_global_device_ids=true | all-gather | bytes 196608 | tf_op jit(solution)/shard_map/all_gather | solution.py:226
  10.0 0.7 broadcast_in_dim.32
  10.8 9.4 %all-to-all-start = ((bf16[8,16,1024]{2,1,0:T(8,128)(2,1)}), bf16[8,16,1024]{2,1,0:T(8,128)(2,1)S(1)}, u32[]{:S(2)}, u32[]{:S(2)}) async-start(bf16[8,16,1024]{2,1,0:T(8,128)(2,1)} %broadcast_in_dim.32), calls=%async_computation | async-start | bytes 524288 | tf_op jit(solution)/shard_map/all_to_all | solution.py:231
  20.2 0.8 copy.5.band_ref
  21.0 0.0 copy-start
  21.0 1.9 %copy-done = bf16[2,4,184,1024]{3,2,1,0:T(8,128)(2,1)S(1)} copy-done((bf16[2,4,184,1024]{3,2,1,0:T(8,128)(2,1)S(1)}, bf16[2,4,184,1024]{3,2,1,0:T(8,128)(2,1)}, u32[]{:S(2)}) %copy-start) | copy-done | bytes 3014680
  22.8 0.6 shard_map.47.resp_ref
  23.5 0.0 copy-done.1
  23.5 0.3 select_reduce_fusion
  23.7 1.4 %convolution_select_fusion.matrix_ref = f32[64,64]{1,0:T(8,128)S(1)} fusion(s32[64]{0:T(128)S(1)} %get-tuple-element.31, s32[64]{0:T(128)S(1)} %get-tuple-element.35, s32[64]{0:T(128)S(1)} %get-tuple-element.32, s32[64]{0:T(128)S(1)} %get-tuple-element.34, s32[64]{0:T(128)S(1)} %get-tuple-element.33, s32[64]{0:T(128)S(1)} %get-tuple-element.36, ...), kind=kOutput, calls=%fused_computation | convolution fusion | flops 28614656 | bytes 18944 | tf_op jit(solution)/shard_map/dot_general | solution.py:249
  25.2 13.2 %all-to-all-done = bf16[8,16,1024]{2,1,0:T(8,128)(2,1)S(1)} async-done(((bf16[8,16,1024]{2,1,0:T(8,128)(2,1)}), bf16[8,16,1024]{2,1,0:T(8,128)(2,1)S(1)}, u32[]{:S(2)}, u32[]{:S(2)}) %all-to-all-start) | async-done | bytes 262176 | tf_op jit(solution)/shard_map/all_to_all | solution.py:231
  38.4 0.1 broadcast_in_dim.36
  38.5 11.8 %all_to_all.30 = bf16[4,128,1024]{2,1,0:T(8,128)(2,1)S(1)} all-to-all(bf16[4,128,1024]{2,1,0:T(8,128)(2,1)S(1)} %broadcast_in_dim.36), channel_id=1, replica_groups=mesh['zh'=8,'zl'=2,'xl'=2,'y'=4,'xh'=2,'c'=2] {'zl','xl'}, dimensions={0} | all-to-all | bytes 2097152 | tf_op jit(solution)/shard_map/all_to_all | solution.py:257
  50.4 1.5 %shard_map.48 = f32[16,48,128]{2,1,0:T(8,128)S(1)} custom-call(bf16[512,1024]{1,0:T(8,128)(2,1)S(1)} %bitcast.9, bf16[2,4,184,1024]{3,2,1,0:T(8,128)(2,1)S(1)} %shard_map.47.resp_ref), custom_call_target="tpu_custom_call" | custom-call | tf_op jit(solution)/shard_map/pallas_call | solution.py:260
  51.8 22.3 %all_to_all.31.parts_ref = f32[16,48,128]{2,1,0:T(8,128)S(1)} all-to-all(f32[16,48,128]{2,1,0:T(8,128)S(1)} %shard_map.48), channel_id=1, replica_groups=mesh['zh'=8,'zl'=2,'xl'=2,'y'=4,'xh'=2,'c'=2] {'y','xh','c'}, dimensions={0} | all-to-all | bytes 786432 | tf_op jit(solution)/shard_map/all_to_all | solution.py:268
  74.1 0.3 shard_map.49
  74.5 11.8 %all_to_all.32.win_ref = bf16[16,48,128]{2,1,0:T(8,128)(2,1)S(1)} all-to-all(bf16[16,48,128]{2,1,0:T(8,128)(2,1)S(1)} %shard_map.49), channel_id=1, replica_groups=mesh['zh'=8,'zl'=2,'xl'=2,'y'=4,'xh'=2,'c'=2] {'y','xh','c'}, dimensions={0} | all-to-all | bytes 393216 | tf_op jit(solution)/shard_map/all_to_all | solution.py:271
  86.3 1.2 shard_map.50
  87.5 15.3 %all_to_all.33.got_ref = bf16[4,128,1024]{2,1,0:T(8,128)(2,1)S(1)} all-to-all(bf16[4,128,1024]{2,1,0:T(8,128)(2,1)S(1)} %bitcast.10), channel_id=1, replica_groups=mesh['zh'=8,'zl'=2,'xl'=2,'y'=4,'xh'=2,'c'=2] {'zl','xl'}, dimensions={0} | all-to-all | bytes 2097152 | tf_op jit(solution)/shard_map/all_to_all | solution.py:281
  102.8 0.1 shard_map.51
  102.9 23.4 %all_to_all.34.got_ref = bf16[8,16,1024]{2,1,0:T(8,128)(2,1)S(1)} all-to-all(bf16[8,16,1024]{2,1,0:T(8,128)(2,1)S(1)} %bitcast.11), channel_id=1, replica_groups=mesh['zh'=8,'zl'=2,'xl'=2,'y'=4,'xh'=2,'c'=2] {'zh'}, dimensions={0} | all-to-all | bytes 524288 | tf_op jit(solution)/shard_map/all_to_all | solution.py:283
  126.3 7.0 %all_gather.11.sums_ref = f32[32,1024]{1,0:T(8,128)S(1)} all-gather(f32[16,1024]{1,0:T(8,128)S(1)} %shard_map.52), channel_id=1, replica_groups=mesh['zh'=8,'zl'=2,'xl'=2,'y'=4,'xh'=2,'c'=2] {'c'}, dimensions={0}, use_global_device_ids=true | all-gather | bytes 196608 | tf_op jit(solution)/shard_map/all_gather | solution.py:285
  133.3 1.3 shard_map.53
  (9 shorter events, 0.1 us)
Async XLA Ops:
  10.8 27.7 %all-to-all-start = ((bf16[8,16,1024]{2,1,0:T(8,128)(2,1)}), bf16[8,16,1024]{2,1,0:T(8,128)(2,1)S(1)}, u32[]{:S(2)}, u32[]{:S(2)}) async-start(bf16[8,16,1024]{2,1,0:T(8,128)(2,1)} %broadcast_in_dim.32), calls=%async_computation | async-start | bytes 524288 | tf_op jit(solution)/shard_map/all_to_all | solution.py:231
  21.0 1.9 %copy-start = (bf16[2,4,184,1024]{3,2,1,0:T(8,128)(2,1)S(1)}, bf16[2,4,184,1024]{3,2,1,0:T(8,128)(2,1)}, u32[]{:S(2)}) copy-start(bf16[2,4,184,1024]{3,2,1,0:T(8,128)(2,1)} %resp_ref.1) | copy-start | bytes 9043972
  22.8 0.7 copy-start.1

commit v6 on v5

--- a/solution.py
+++ b/solution.py
@@ -46,19 +46,40 @@
     )
 
 
+def far_order(count):
+    step = 1 if count % 3 == 0 else 3
+    return [step * j % count for j in range(count)]
+
+
+def far_all_to_all(x):
+    axes = SRC + RCV + ("c",)
+    zh, *rest = (lax.axis_size(a) for a in axes)
+    apart = math.prod(rest)
+    groups = [[j * apart + i for j in far_order(zh)] for i in range(apart)]
+    return lax.all_to_all(x, axes, 0, 0, tiled=True, axis_index_groups=groups)
+
+
 def spectra_body(f_ref, own_ref, other_ref, last_ref, held_ref, sem_ref):
-    copy = pltpu.make_async_copy(f_ref, held_ref, sem_ref)
-    copy.start()
     steps, focal, cols = f_ref.shape
+    pieces = sem_ref.shape[0]
+    block = steps // pieces
+    copies = []
+    for i in range(pieces):
+        at = pl.ds(i * block, block)
+        copies.append(pltpu.make_async_copy(f_ref.at[at], held_ref.at[at], sem_ref.at[i]))
+        copies[-1].start()
     core = lax.axis_index("c")
     table = focal_table((core, 1 - core), core, steps, focal, 1.0 / math.sqrt(NT))
     rows = table.shape[0]
     table = jnp.concatenate(thirds(table), 0)
     high, middle, low = thirds(focal_table((0, 1), core, steps, focal, 1.0 / math.sqrt(FREQ)))
     last_ref[...] = jnp.concatenate([high, high, middle, high, low, middle], 0)
-    copy.wait()
-    merged = held_ref[...].reshape(steps * focal, cols)
-    sums = jnp.dot(table, merged, preferred_element_type=F32)
+    sums = 0.0
+    for i, copy in enumerate(copies):
+        copy.wait()
+        merged = held_ref[i * block : (i + 1) * block].reshape(block * focal, cols)
+        left = table[:, i * block * focal : (i + 1) * block * focal]
+        sums += jnp.dot(left, merged, preferred_element_type=F32)
     sums = sums[:rows] + sums[rows : 2 * rows] + sums[2 * rows :]
     own_ref[...] = sums[: rows // 2]
     other_ref[...] = sums[rows // 2 :]
@@ -220,7 +241,7 @@
         out_shape=[struct((own_rows, cols), F32)] * 2
         + [struct((6 * 2 * own_rows, steps * focal_here), BF16)],
         in_specs=[pl.BlockSpec(memory_space=pltpu.HBM)],
-        scratch_shapes=[pltpu.VMEM(f_time.shape, BF16), pltpu.SemaphoreType.DMA],
+        scratch_shapes=[pltpu.VMEM(f_time.shape, BF16), pltpu.SemaphoreType.DMA((4,))],
         compiler_params=pltpu.CompilerParams(vmem_limit_bytes=54784 << 10),
     )(f_time)
     others = lax.all_gather(other, "c", axis=0)
@@ -228,7 +249,7 @@
     other = jnp.where(core == 0, others[1], others[0])
     spectra = (own + other).astype(BF16)
     near = jnp.broadcast_to(spectra[None], (zh, own_rows, cols))
-    near = lax.all_to_all(near, "zh", 0, 0, tiled=True).reshape(zh * own_rows, cols)
+    near = far_all_to_all(near).reshape(zh * own_rows, cols)
 
     masked = vmem_call(
         masked_body,
@@ -243,7 +264,8 @@
     waves = wave(row // part_rows * HALF + row % HALF, row // HALF % 2, col)
     point = (lax.axis_index(RCV) * 2 + core) * part_focal + iota((2 * part_rows, focal), 0) // ROWS % part_focal
     block = point // focal_here
-    point = (block % zh * pairs + block // zh) * focal_here + point % focal_here
+    far = block % zh * far_order(zh)[1] % zh
+    point = (far * pairs + block // zh) * focal_here + point % focal_here
     window = jnp.where(point == iota((2 * part_rows, focal), 1), gates[None, :], 0).sum(1)
     inner = jnp.where(col < window[:, None], waves / math.sqrt(NT), 0.0)
     matrix = lax.dot_general(
@@ -280,7 +302,7 @@
     )(windowed, masked)
     got = lax.all_to_all(sends.reshape(pairs, zh * own_rows, cols), PAIR, 0, 0, tiled=True)
     got = vmem_call(sum_body, struct((zh * own_rows, cols), BF16))(got)
-    got = lax.all_to_all(got.reshape(zh, own_rows, cols), "zh", 0, 0, tiled=True)
+    got = far_all_to_all(got.reshape(zh, own_rows, cols))
     got = vmem_call(sum_body, struct((own_rows, cols), F32))(got)
     both = lax.all_gather(got, "c", axis=0, tiled=True)
 
@@ -289,7 +311,7 @@
         out_shape=struct((steps, focal_here, cols), BF16),
         in_specs=[pl.BlockSpec(memory_space=pltpu.VMEM)] * 2,
         out_specs=pl.BlockSpec(memory_space=pltpu.HBM),
-        scratch_shapes=[pltpu.VMEM(f_time.shape, BF16), pltpu.SemaphoreType.DMA((2,))],
+        scratch_shapes=[pltpu.VMEM(f_time.shape, BF16), pltpu.SemaphoreType.DMA((4,))],
         compiler_params=pltpu.CompilerParams(vmem_limit_bytes=12 << 20),
     )(table, both)
 

time: 135 us -> 133 us (0.985)
    all_to_all x1, blocking collectives: 11.8 us -> 14.5 us  [shards(): lax.all_to_all(every, PAIR, 0, 0, tiled=True).reshape(focal * ROWS, cols)]
    all_to_all x1, blocking collectives: 22.3 us -> 19.9 us  [shards(): parts = lax.all_to_all(parts, RCV + ('c',), 0, 0, tiled=True)]
    all_gather x1, blocking collectives: 7 us -> 5.37 us  [shards(): both = lax.all_gather(got, 'c', axis=0, tiled=True)]
where the time goes in v6:
time: 133 us; the launch traced here: 132 us
  blocking collectives  98.8 us (74%)
  waiting for transfers between devices  12.4 us (9%)
  starting transfers between devices  9.44 us (7%)
  Pallas kernels  6.49 us (5%)
  local copies, waits for them, and re-layouts  3.5 us (3%)
  matrix products  1.44 us (1%)
    all_to_all x1, blocking collectives, far_all_to_all(): return lax.all_to_all(x, axes, 0, 0, tiled=True, axis_index_groups=groups)  23.5 us
    all_to_all x1, blocking collectives, shards(): parts = lax.all_to_all(parts, RCV + ('c',), 0, 0, tiled=True)  19.9 us
    all_to_all x1, blocking collectives, shards(): lax.all_to_all(sends.reshape(pairs, zh * own_rows, cols), PAIR, 0, 0, til...  15.3 us
    all_to_all x1, blocking collectives, shards(): lax.all_to_all(every, PAIR, 0, 0, tiled=True).reshape(focal * ROWS, cols)  14.5 us
    all_to_all x1, waiting for transfers between devices, far_all_to_all(): return lax.all_to_all(x, axes, 0, 0, tiled=True, axis_index_groups=groups)  12.4 us
    all_to_all x1, blocking collectives, shards(): windowed = lax.all_to_all(gated, RCV + ('c',), 0, 0, tiled=True)  11.8 us
    all_to_all x1, starting transfers between devices, far_all_to_all(): return lax.all_to_all(x, axes, 0, 0, tiled=True, axis_index_groups=groups)  9.44 us
    all_gather x1, blocking collectives, shards(): others = lax.all_gather(other, 'c', axis=0)  8.42 us
  transfers between devices with their start and end apart: 1, of which 1 were waited for; matrix products, arithmetic and copies ran while one was open for 2% of the time, Pallas kernels for 0%

profile of v6, /device:TPU:1, one launch (start us, length us, event | category | flops | bytes accessed | tf_op | source)
XLA Modules:
  0.0 132.4 jit_solution(14672226337076312195)
XLA Ops:
  0.0 1.5 %shard_map.46 = (f32[16,1024]{1,0:T(8,128)S(1)}, f32[16,1024]{1,0:T(8,128)S(1)}, bf16[192,512]{1,0:T(8,128)(2,1)S(1)}) custom-call(bf16[256,2,1024]{2,1,0:T(2,128)(2,1)} %f_ref.1), custom_call_target="tpu_custom_call" | custom-call | tf_op jit(solution)/shard_map/pallas_call | solution.py:239
  1.5 8.4 %all-gather = f32[32,1024]{1,0:T(8,128)S(1)} all-gather(f32[16,1024]{1,0:T(8,128)S(1)} %get-tuple-element.17), channel_id=2, replica_groups=mesh['zh'=8,'zl'=2,'xl'=2,'y'=4,'xh'=2,'c'=2] {'c'}, dimensions={0}, use_global_device_ids=true | all-gather | bytes 196608 | tf_op jit(solution)/shard_map/all_gather | solution.py:247
  10.0 0.7 broadcast_in_dim.32
  10.7 9.4 %all-to-all-start = ((bf16[8,16,1024]{2,1,0:T(8,128)(2,1)}), bf16[8,16,1024]{2,1,0:T(8,128)(2,1)S(1)}, u32[]{:S(2)}, u32[]{:S(2)}) async-start(bf16[8,16,1024]{2,1,0:T(8,128)(2,1)} %broadcast_in_dim.32), calls=%async_computation | async-start | bytes 524288 | tf_op jit(solution)/shard_map/all_to_all | solution.py:59
  20.2 0.8 copy.5.band_ref
  20.9 0.0 copy-start
  20.9 1.9 %copy-done = bf16[2,4,184,1024]{3,2,1,0:T(8,128)(2,1)S(1)} copy-done((bf16[2,4,184,1024]{3,2,1,0:T(8,128)(2,1)S(1)}, bf16[2,4,184,1024]{3,2,1,0:T(8,128)(2,1)}, u32[]{:S(2)}) %copy-start) | copy-done | bytes 3014680
  22.8 0.6 shard_map.47.resp_ref
  23.4 0.0 copy-done.1
  23.4 0.3 select_reduce_fusion
  23.7 1.4 %convolution_select_fusion.matrix_ref = f32[64,64]{1,0:T(8,128)S(1)} fusion(s32[64]{0:T(128)S(1)} %get-tuple-element.31, s32[64]{0:T(128)S(1)} %get-tuple-element.35, s32[64]{0:T(128)S(1)} %get-tuple-element.32, s32[64]{0:T(128)S(1)} %get-tuple-element.34, s32[64]{0:T(128)S(1)} %get-tuple-element.33, s32[64]{0:T(128)S(1)} %get-tuple-element.36, ...), kind=kOutput, calls=%fused_computation | convolution fusion | flops 28614656 | bytes 18944 | tf_op jit(solution)/shard_map/dot_general | solution.py:271
  25.2 12.4 %all-to-all-done = bf16[8,16,1024]{2,1,0:T(8,128)(2,1)S(1)} async-done(((bf16[8,16,1024]{2,1,0:T(8,128)(2,1)}), bf16[8,16,1024]{2,1,0:T(8,128)(2,1)S(1)}, u32[]{:S(2)}, u32[]{:S(2)}) %all-to-all-start) | async-done | bytes 262176 | tf_op jit(solution)/shard_map/all_to_all | solution.py:59
  37.5 0.1 broadcast_in_dim.36
  37.6 14.5 %all_to_all.30 = bf16[4,128,1024]{2,1,0:T(8,128)(2,1)S(1)} all-to-all(bf16[4,128,1024]{2,1,0:T(8,128)(2,1)S(1)} %broadcast_in_dim.36), channel_id=1, replica_groups=mesh['zh'=8,'zl'=2,'xl'=2,'y'=4,'xh'=2,'c'=2] {'zl','xl'}, dimensions={0} | all-to-all | bytes 2097152 | tf_op jit(solution)/shard_map/all_to_all | solution.py:279
  52.2 1.5 %shard_map.48 = f32[16,48,128]{2,1,0:T(8,128)S(1)} custom-call(bf16[512,1024]{1,0:T(8,128)(2,1)S(1)} %bitcast.9, bf16[2,4,184,1024]{3,2,1,0:T(8,128)(2,1)S(1)} %shard_map.47.resp_ref), custom_call_target="tpu_custom_call" | custom-call | tf_op jit(solution)/shard_map/pallas_call | solution.py:282
  53.6 19.9 %all_to_all.31.parts_ref = f32[16,48,128]{2,1,0:T(8,128)S(1)} all-to-all(f32[16,48,128]{2,1,0:T(8,128)S(1)} %shard_map.48), channel_id=1, replica_groups=mesh['zh'=8,'zl'=2,'xl'=2,'y'=4,'xh'=2,'c'=2] {'y','xh','c'}, dimensions={0} | all-to-all | bytes 786432 | tf_op jit(solution)/shard_map/all_to_all | solution.py:290
  73.5 0.3 shard_map.49
  73.8 11.8 %all_to_all.32.win_ref = bf16[16,48,128]{2,1,0:T(8,128)(2,1)S(1)} all-to-all(bf16[16,48,128]{2,1,0:T(8,128)(2,1)S(1)} %shard_map.49), channel_id=1, replica_groups=mesh['zh'=8,'zl'=2,'xl'=2,'y'=4,'xh'=2,'c'=2] {'y','xh','c'}, dimensions={0} | all-to-all | bytes 393216 | tf_op jit(solution)/shard_map/all_to_all | solution.py:293
  85.6 1.2 shard_map.50
  86.8 15.3 %all_to_all.33.got_ref = bf16[4,128,1024]{2,1,0:T(8,128)(2,1)S(1)} all-to-all(bf16[4,128,1024]{2,1,0:T(8,128)(2,1)S(1)} %bitcast.10), channel_id=1, replica_groups=mesh['zh'=8,'zl'=2,'xl'=2,'y'=4,'xh'=2,'c'=2] {'zl','xl'}, dimensions={0} | all-to-all | bytes 2097152 | tf_op jit(solution)/shard_map/all_to_all | solution.py:303
  102.1 0.1 shard_map.51
  102.2 23.5 %all_to_all.34.got_ref = bf16[8,16,1024]{2,1,0:T(8,128)(2,1)S(1)} all-to-all(bf16[8,16,1024]{2,1,0:T(8,128)(2,1)S(1)} %bitcast.11), channel_id=1, replica_groups={{0,192,384,64,256,448,128,320},{1,193,385,65,257,449,129,321},{2,194,38..., dimensions={0} | all-to-all | bytes 524288 | tf_op jit(solution)/shard_map/all_to_all | solution.py:59
  125.8 5.4 %all_gather.11.sums_ref = f32[32,1024]{1,0:T(8,128)S(1)} all-gather(f32[16,1024]{1,0:T(8,128)S(1)} %shard_map.52), channel_id=1, replica_groups=mesh['zh'=8,'zl'=2,'xl'=2,'y'=4,'xh'=2,'c'=2] {'c'}, dimensions={0}, use_global_device_ids=true | all-gather | bytes 196608 | tf_op jit(solution)/shard_map/all_gather | solution.py:307
  131.2 1.3 shard_map.53
  (9 shorter events, 0.1 us)
Async XLA Ops:
  10.7 26.8 %all-to-all-start = ((bf16[8,16,1024]{2,1,0:T(8,128)(2,1)}), bf16[8,16,1024]{2,1,0:T(8,128)(2,1)S(1)}, u32[]{:S(2)}, u32[]{:S(2)}) async-start(bf16[8,16,1024]{2,1,0:T(8,128)(2,1)} %broadcast_in_dim.32), calls=%async_computation | async-start | bytes 524288 | tf_op jit(solution)/shard_map/all_to_all | solution.py:59
  20.9 1.9 %copy-start = (bf16[2,4,184,1024]{3,2,1,0:T(8,128)(2,1)S(1)}, bf16[2,4,184,1024]{3,2,1,0:T(8,128)(2,1)}, u32[]{:S(2)}) copy-start(bf16[2,4,184,1024]{3,2,1,0:T(8,128)(2,1)} %resp_ref.1) | copy-start | bytes 9043972
  22.8 0.7 copy-start.1

commit v7 on v6

--- a/solution.py
+++ b/solution.py
@@ -47,7 +47,7 @@
 
 
 def far_order(count):
-    step = 1 if count % 3 == 0 else 3
+    step = 1 if count % 5 == 0 else 5
     return [step * j % count for j in range(count)]
 
 
@@ -85,19 +85,49 @@
     other_ref[...] = sums[rows // 2 :]
 
 
-def masked_body(band_ref, resp_ref, out_ref):
-    band = band_ref[...].astype(F32).astype(BF16)
-    down, across = band.shape
+def local_body(band_ref, gates_ref, resp_ref, masked_ref, matrix_ref):
+    across, down = band_ref.shape
     parts, _, sources, cols = resp_ref.shape
     shape = (across, cols)
     picks = (iota(shape, 0) == iota(shape, 1) // (cols // across)).astype(F32).astype(BF16)
-    wide = jnp.dot(band, picks, preferred_element_type=F32).astype(BF16)
+    band = band_ref[...].astype(F32).astype(BF16)
+    dims = (((0,), (0,)), ((), ()))
+    wide = lax.dot_general(band, picks, dims, preferred_element_type=F32).astype(BF16)
     shape = (sources, down)
     picks = (iota(shape, 0) // (sources // down) == iota(shape, 1)).astype(F32).astype(BF16)
     mask = jnp.dot(picks, wide, preferred_element_type=F32).astype(BF16)
     for c in range(parts):
         for k in range(HALF):
-            out_ref[c, k] = resp_ref[c, k] * mask
+            masked_ref[c, k] = resp_ref[c, k] * mask
+
+    zh, zl, xl = (lax.axis_size(a) for a in SRC)
+    focal = gates_ref.shape[1]
+    pairs, focal_here = zl * xl, focal // (zh * zl * xl)
+    rows = matrix_ref.shape[0]
+    part_focal = rows // (2 * ROWS)
+    shape = (rows, NT)
+    row, col = iota(shape, 0), iota(shape, 1)
+    waves = wave(row // (rows // 2) * HALF + row % HALF, row // HALF % 2, col)
+    chunk = lax.axis_index("y") * lax.axis_size("xh") + lax.axis_index("xh")
+    chunk = chunk * 2 + lax.axis_index("c")
+    shape = (rows, focal)
+    point = chunk * part_focal + iota(shape, 0) // ROWS % part_focal
+    block = point // focal_here
+    far = block % zh * far_order(zh)[1] % zh
+    point = (far * pairs + block // zh) * focal_here + point % focal_here
+    own = jnp.where(point == iota(shape, 1), gates_ref[...].astype(F32), 0.0)
+    window = jnp.sum(own, 1, keepdims=True)
+    inner = jnp.where(col.astype(F32) < window, waves / math.sqrt(NT), 0.0)
+    matrix = lax.dot_general(
+        inner,
+        waves * (2.0 / math.sqrt(NT)),
+        (((1,), (1,)), ((), ())),
+        precision=HIGHEST,
+        preferred_element_type=F32,
+    )
+    shape = matrix.shape
+    same = iota(shape, 0) // ROWS % part_focal == iota(shape, 1) // ROWS % part_focal
+    matrix_ref[...] = jnp.where(same, matrix, 0.0)
 
 
 def forward_body(spec_ref, resp_ref, out_ref, wide_ref, sums_ref):
@@ -245,38 +275,17 @@
         compiler_params=pltpu.CompilerParams(vmem_limit_bytes=54784 << 10),
     )(f_time)
     others = lax.all_gather(other, "c", axis=0)
-    others, core, gates, band_map = lax.optimization_barrier((others, core, gates, band_map))
     other = jnp.where(core == 0, others[1], others[0])
     spectra = (own + other).astype(BF16)
     near = jnp.broadcast_to(spectra[None], (zh, own_rows, cols))
     near = far_all_to_all(near).reshape(zh * own_rows, cols)
-
-    masked = vmem_call(
-        masked_body,
-        struct(reflect.shape, BF16),
-        cost=pl.CostEstimate(flops=reflect.size, transcendentals=0, bytes_accessed=4 * reflect.size),
-    )(band_map, reflect)
-
-    part_rows = focal * ROWS // chunks
-    part_focal = part_rows // ROWS
-    shape = (2 * part_rows, NT)
-    row, col = iota(shape, 0), iota(shape, 1)
-    waves = wave(row // part_rows * HALF + row % HALF, row // HALF % 2, col)
-    point = (lax.axis_index(RCV) * 2 + core) * part_focal + iota((2 * part_rows, focal), 0) // ROWS % part_focal
-    block = point // focal_here
-    far = block % zh * far_order(zh)[1] % zh
-    point = (far * pairs + block // zh) * focal_here + point % focal_here
-    window = jnp.where(point == iota((2 * part_rows, focal), 1), gates[None, :], 0).sum(1)
-    inner = jnp.where(col < window[:, None], waves / math.sqrt(NT), 0.0)
-    matrix = lax.dot_general(
-        inner, waves * (2.0 / math.sqrt(NT)), (((1,), (1,)), ((), ())), precision=HIGHEST
-    )
-    shape = matrix.shape
-    same = iota(shape, 0) // ROWS % part_focal == iota(shape, 1) // ROWS % part_focal
-    matrix = jnp.where(same, matrix, 0.0)
-    near, masked, matrix = lax.optimization_barrier((near, masked, matrix))
     every = jnp.broadcast_to(near[None], (pairs, zh * own_rows, cols))
     every = lax.all_to_all(every, PAIR, 0, 0, tiled=True).reshape(focal * ROWS, cols)
+    every, gates, band_map = lax.optimization_barrier((every, gates, band_map))
+    part_rows = focal * ROWS // chunks
+    masked, matrix = vmem_call(
+        local_body, [struct(reflect.shape, BF16), struct((2 * part_rows, 2 * part_rows), F32)]
+    )(band_map.T, gates.reshape(1, focal), reflect)
 
     packed = part_rows * 3 // 2
     parts = vmem_call(

time: 133 us -> 135 us (1.015)
  blocking collectives: 98.8 us -> 127 us
  waiting for transfers between devices: 12.4 us -> 0 us
  starting transfers between devices: 9.44 us -> 0 us
  local copies, waits for them, and re-layouts: 3.5 us -> 0.15 us
  matrix products: 1.44 us -> 0 us
    all_to_all x1 -> x2, blocking collectives: 23.5 us -> 50.8 us  [far_all_to_all(): return lax.all_to_all(x, axes, 0, 0, tiled=True, axis_index_groups=groups)]
    all_to_all x1 -> x0, waiting for transfers between devices: 12.4 us -> none  [far_all_to_all(): return lax.all_to_all(x, axes, 0, 0, tiled=True, axis_index_groups=groups)]
    all_to_all x1 -> x0, starting transfers between devices: 9.44 us -> none  [far_all_to_all(): return lax.all_to_all(x, axes, 0, 0, tiled=True, axis_index_groups=groups)]
    all_to_all x1, blocking collectives: 14.5 us -> 11.8 us  [shards(): lax.all_to_all(every, PAIR, 0, 0, tiled=True).reshape(focal * ROWS, cols)]
    all_to_all x1, blocking collectives: 19.9 us -> 22.3 us  [shards(): parts = lax.all_to_all(parts, RCV + ('c',), 0, 0, tiled=True)]
    unnamed x4 -> x6, local copies, waits for them, and re-layouts: 1.88 us -> 0.01 us
    all_gather x1, blocking collectives: 5.37 us -> 6.99 us  [shards(): both = lax.all_gather(got, 'c', axis=0, tiled=True)]
    dot_general x1 -> x0, matrix products: 1.44 us -> none  [shards(): lax.dot_general(inner, waves * (2.0 / math.sqrt(NT)), (((1,), (1,)), ((),...]
  transfers between devices with their start and end apart: 1 -> 0, of which waited for: 1 -> 0; matrix products, arithmetic and copies ran while one was open for 2% -> 0% of each run, Pallas kernels for 0% -> 0%
where the time goes in v7:
time: 135 us
  blocking collectives  127 us (94%)
  Pallas kernels  7.24 us (5%)
    all_to_all x2, blocking collectives, far_all_to_all(): return lax.all_to_all(x, axes, 0, 0, tiled=True, axis_index_groups=groups)  50.8 us
    all_to_all x1, blocking collectives, shards(): parts = lax.all_to_all(parts, RCV + ('c',), 0, 0, tiled=True)  22.3 us
    all_to_all x1, blocking collectives, shards(): lax.all_to_all(sends.reshape(pairs, zh * own_rows, cols), PAIR, 0, 0, til...  15.3 us
    all_to_all x1, blocking collectives, shards(): lax.all_to_all(every, PAIR, 0, 0, tiled=True).reshape(focal * ROWS, cols)  11.8 us
    all_to_all x1, blocking collectives, shards(): windowed = lax.all_to_all(gated, RCV + ('c',), 0, 0, tiled=True)  11.8 us
    all_gather x1, blocking collectives, shards(): others = lax.all_gather(other, 'c', axis=0)  8.43 us
    all_gather x1, blocking collectives, shards(): both = lax.all_gather(got, 'c', axis=0, tiled=True)  6.99 us

profile of v7, /device:TPU:1, one launch (start us, length us, event | category | flops | bytes accessed | tf_op | source)
XLA Modules:
  0.0 134.9 jit_solution(14451351654584634914)
XLA Ops:
  0.0 0.0 copy-start.2
  0.0 0.0 copy-start.1
  0.0 0.0 copy-start
  0.0 1.7 %shard_map.46 = (f32[16,1024]{1,0:T(8,128)S(1)}, f32[16,1024]{1,0:T(8,128)S(1)}, bf16[192,512]{1,0:T(8,128)(2,1)S(1)}) custom-call(bf16[256,2,1024]{2,1,0:T(2,128)(2,1)} %f_ref.1), custom_call_target="tpu_custom_call" | custom-call | tf_op jit(solution)/shard_map/pallas_call | solution.py:269
  1.7 8.4 %all-gather = f32[32,1024]{1,0:T(8,128)S(1)} all-gather(f32[16,1024]{1,0:T(8,128)S(1)} %get-tuple-element.15), channel_id=2, replica_groups=mesh['zh'=8,'zl'=2,'xl'=2,'y'=4,'xh'=2,'c'=2] {'c'}, dimensions={0}, use_global_device_ids=true | all-gather | bytes 196608 | tf_op jit(solution)/shard_map/all_gather | solution.py:277
  10.2 27.5 %all_to_all.30 = bf16[8,16,1024]{2,1,0:T(8,128)(2,1)S(1)} all-to-all(bf16[8,16,1024]{2,1,0:T(8,128)(2,1)S(1)} %broadcast_in_dim.6), channel_id=1, replica_groups={{0,320,128,448,256,64,384,192},{1,321,129,449,257,65,385,193},{2,322,13..., dimensions={0} | all-to-all | bytes 524288 | tf_op jit(solution)/shard_map/all_to_all | solution.py:59
  37.6 0.1 broadcast_in_dim.15
  37.8 11.8 %all_to_all.31 = bf16[4,128,1024]{2,1,0:T(8,128)(2,1)S(1)} all-to-all(bf16[4,128,1024]{2,1,0:T(8,128)(2,1)S(1)} %broadcast_in_dim.15), channel_id=1, replica_groups=mesh['zh'=8,'zl'=2,'xl'=2,'y'=4,'xh'=2,'c'=2] {'zl','xl'}, dimensions={0} | all-to-all | bytes 2097152 | tf_op jit(solution)/shard_map/all_to_all | solution.py:283
  49.6 0.0 copy-done.2
  49.6 0.0 copy-done.1
  49.6 0.0 copy-done
  49.6 1.1 shard_map.47
  50.7 1.5 %shard_map.48 = f32[16,48,128]{2,1,0:T(8,128)S(1)} custom-call(bf16[512,1024]{1,0:T(8,128)(2,1)S(1)} %bitcast.6, bf16[2,4,184,1024]{3,2,1,0:T(8,128)(2,1)S(1)} %get-tuple-element.20.resp_ref), custom_call_target="tpu_custom_call" | custom-call | tf_op jit(solution)/shard_map/pallas_call | solution.py:291
  52.2 22.3 %all_to_all.32.parts_ref = f32[16,48,128]{2,1,0:T(8,128)S(1)} all-to-all(f32[16,48,128]{2,1,0:T(8,128)S(1)} %shard_map.48), channel_id=1, replica_groups=mesh['zh'=8,'zl'=2,'xl'=2,'y'=4,'xh'=2,'c'=2] {'y','xh','c'}, dimensions={0} | all-to-all | bytes 786432 | tf_op jit(solution)/shard_map/all_to_all | solution.py:299
  74.5 0.3 shard_map.49
  74.9 11.8 %all_to_all.33.win_ref = bf16[16,48,128]{2,1,0:T(8,128)(2,1)S(1)} all-to-all(bf16[16,48,128]{2,1,0:T(8,128)(2,1)S(1)} %shard_map.49), channel_id=1, replica_groups=mesh['zh'=8,'zl'=2,'xl'=2,'y'=4,'xh'=2,'c'=2] {'y','xh','c'}, dimensions={0} | all-to-all | bytes 393216 | tf_op jit(solution)/shard_map/all_to_all | solution.py:302
  86.7 1.2 shard_map.50
  87.9 15.3 %all_to_all.34.got_ref = bf16[4,128,1024]{2,1,0:T(8,128)(2,1)S(1)} all-to-all(bf16[4,128,1024]{2,1,0:T(8,128)(2,1)S(1)} %bitcast.7), channel_id=1, replica_groups=mesh['zh'=8,'zl'=2,'xl'=2,'y'=4,'xh'=2,'c'=2] {'zl','xl'}, dimensions={0} | all-to-all | bytes 2097152 | tf_op jit(solution)/shard_map/all_to_all | solution.py:312
  103.2 0.1 shard_map.51
  103.3 23.3 %all_to_all.35.got_ref = bf16[8,16,1024]{2,1,0:T(8,128)(2,1)S(1)} all-to-all(bf16[8,16,1024]{2,1,0:T(8,128)(2,1)S(1)} %bitcast.8), channel_id=1, replica_groups={{0,320,128,448,256,64,384,192},{1,321,129,449,257,65,385,193},{2,322,13..., dimensions={0} | all-to-all | bytes 524288 | tf_op jit(solution)/shard_map/all_to_all | solution.py:59
  126.7 7.0 %all_gather.11.sums_ref = f32[32,1024]{1,0:T(8,128)S(1)} all-gather(f32[16,1024]{1,0:T(8,128)S(1)} %shard_map.52), channel_id=1, replica_groups=mesh['zh'=8,'zl'=2,'xl'=2,'y'=4,'xh'=2,'c'=2] {'c'}, dimensions={0}, use_global_device_ids=true | all-gather | bytes 196608 | tf_op jit(solution)/shard_map/all_gather | solution.py:316
  133.7 1.3 shard_map.53
  (3 shorter events, 0.1 us)
Async XLA Ops:
  0.0 49.6 %copy-start.2 = (s32[64]{0:T(128)S(1)}, s32[64]{0:T(128)}, u32[]{:S(2)}) copy-start(s32[64]{0:T(128)} %param.7) | copy-start | bytes 772
  0.0 49.6 %copy-start.1 = (s32[23,4]{0,1:T(4,128)S(1)}, s32[23,4]{0,1:T(4,128)}, u32[]{:S(2)}) copy-start(s32[23,4]{0,1:T(4,128)} %param.6) | copy-start | bytes 1108
  0.0 49.6 %copy-start = (bf16[2,4,184,1024]{3,2,1,0:T(8,128)(2,1)S(1)}, bf16[2,4,184,1024]{3,2,1,0:T(8,128)(2,1)}, u32[]{:S(2)}) copy-start(bf16[2,4,184,1024]{3,2,1,0:T(8,128)(2,1)} %resp_ref.1) | copy-start | bytes 9043972

commit v8 on v6

--- a/solution.py
+++ b/solution.py
@@ -47,8 +47,7 @@
 
 
 def far_order(count):
-    step = 1 if count % 3 == 0 else 3
-    return [step * j % count for j in range(count)]
+    return sorted(range(count), key=lambda j: (min(j, count - j), j))
 
 
 def far_all_to_all(x):
@@ -264,7 +263,7 @@
     waves = wave(row // part_rows * HALF + row % HALF, row // HALF % 2, col)
     point = (lax.axis_index(RCV) * 2 + core) * part_focal + iota((2 * part_rows, focal), 0) // ROWS % part_focal
     block = point // focal_here
-    far = block % zh * far_order(zh)[1] % zh
+    far = sum(jnp.where(block % zh == j, f, 0) for j, f in enumerate(far_order(zh)))
     point = (far * pairs + block // zh) * focal_here + point % focal_here
     window = jnp.where(point == iota((2 * part_rows, focal), 1), gates[None, :], 0).sum(1)
     inner = jnp.where(col < window[:, None], waves / math.sqrt(NT), 0.0)

time: 133 us -> 135 us (1.015)
  blocking collectives: 98.8 us -> 101 us
    all_to_all x1, blocking collectives: 14.5 us -> 11.2 us  [shards(): lax.all_to_all(every, PAIR, 0, 0, tiled=True).reshape(focal * ROWS, cols)]
    all_to_all x1, blocking collectives: 19.9 us -> 22.9 us  [shards(): parts = lax.all_to_all(parts, RCV + ('c',), 0, 0, tiled=True)]
    all_gather x1, blocking collectives: 5.37 us -> 6.92 us  [shards(): both = lax.all_gather(got, 'c', axis=0, tiled=True)]
where the time goes in v8:
time: 135 us
  blocking collectives  101 us (75%)
  waiting for transfers between devices  12.7 us (9%)
  starting transfers between devices  9.44 us (7%)
  Pallas kernels  6.51 us (5%)
  local copies, waits for them, and re-layouts  3.5 us (3%)
  matrix products  1.44 us (1%)
    all_to_all x1, blocking collectives, far_all_to_all(): return lax.all_to_all(x, axes, 0, 0, tiled=True, axis_index_groups=groups)  24.2 us
    all_to_all x1, blocking collectives, shards(): parts = lax.all_to_all(parts, RCV + ('c',), 0, 0, tiled=True)  22.9 us
    all_to_all x1, blocking collectives, shards(): lax.all_to_all(sends.reshape(pairs, zh * own_rows, cols), PAIR, 0, 0, til...  15.3 us
    all_to_all x1, waiting for transfers between devices, far_all_to_all(): return lax.all_to_all(x, axes, 0, 0, tiled=True, axis_index_groups=groups)  12.7 us
    all_to_all x1, blocking collectives, shards(): windowed = lax.all_to_all(gated, RCV + ('c',), 0, 0, tiled=True)  11.8 us
    all_to_all x1, blocking collectives, shards(): lax.all_to_all(every, PAIR, 0, 0, tiled=True).reshape(focal * ROWS, cols)  11.2 us
    all_to_all x1, starting transfers between devices, far_all_to_all(): return lax.all_to_all(x, axes, 0, 0, tiled=True, axis_index_groups=groups)  9.44 us
    all_gather x1, blocking collectives, shards(): others = lax.all_gather(other, 'c', axis=0)  8.42 us
  transfers between devices with their start and end apart: 1, of which 1 were waited for; matrix products, arithmetic and copies ran while one was open for 2% of the time, Pallas kernels for 0%

profile of v8, /device:TPU:1, one launch (start us, length us, event | category | flops | bytes accessed | tf_op | source)
XLA Modules:
  0.0 134.8 jit_solution(4181004618070227463)
XLA Ops:
  0.0 1.5 %shard_map.46 = (f32[16,1024]{1,0:T(8,128)S(1)}, f32[16,1024]{1,0:T(8,128)S(1)}, bf16[192,512]{1,0:T(8,128)(2,1)S(1)}) custom-call(bf16[256,2,1024]{2,1,0:T(2,128)(2,1)} %f_ref.1), custom_call_target="tpu_custom_call" | custom-call | tf_op jit(solution)/shard_map/pallas_call | solution.py:238
  1.5 8.4 %all-gather = f32[32,1024]{1,0:T(8,128)S(1)} all-gather(f32[16,1024]{1,0:T(8,128)S(1)} %get-tuple-element.17), channel_id=2, replica_groups=mesh['zh'=8,'zl'=2,'xl'=2,'y'=4,'xh'=2,'c'=2] {'c'}, dimensions={0}, use_global_device_ids=true | all-gather | bytes 196608 | tf_op jit(solution)/shard_map/all_gather | solution.py:246
  10.0 0.7 broadcast_in_dim.52
  10.7 9.4 %all-to-all-start = ((bf16[8,16,1024]{2,1,0:T(8,128)(2,1)}), bf16[8,16,1024]{2,1,0:T(8,128)(2,1)S(1)}, u32[]{:S(2)}, u32[]{:S(2)}) async-start(bf16[8,16,1024]{2,1,0:T(8,128)(2,1)} %broadcast_in_dim.52), calls=%async_computation | async-start | bytes 524288 | tf_op jit(solution)/shard_map/all_to_all | solution.py:58
  20.2 0.8 copy.5.band_ref
  20.9 0.0 copy-start
  20.9 1.9 %copy-done = bf16[2,4,184,1024]{3,2,1,0:T(8,128)(2,1)S(1)} copy-done((bf16[2,4,184,1024]{3,2,1,0:T(8,128)(2,1)S(1)}, bf16[2,4,184,1024]{3,2,1,0:T(8,128)(2,1)}, u32[]{:S(2)}) %copy-start) | copy-done | bytes 3014680
  22.8 0.6 shard_map.47.resp_ref
  23.4 0.0 copy-done.1
  23.4 0.3 select_reduce_fusion
  23.7 1.4 %convolution_select_fusion.matrix_ref = f32[64,64]{1,0:T(8,128)S(1)} fusion(s32[64]{0:T(128)S(1)} %get-tuple-element.31, s32[64]{0:T(128)S(1)} %get-tuple-element.35, s32[64]{0:T(128)S(1)} %get-tuple-element.32, s32[64]{0:T(128)S(1)} %get-tuple-element.34, s32[64]{0:T(128)S(1)} %get-tuple-element.33, s32[64]{0:T(128)S(1)} %get-tuple-element.36, ...), kind=kOutput, calls=%fused_computation | convolution fusion | flops 28614656 | bytes 18944 | tf_op jit(solution)/shard_map/dot_general | solution.py:270
  25.2 12.7 %all-to-all-done = bf16[8,16,1024]{2,1,0:T(8,128)(2,1)S(1)} async-done(((bf16[8,16,1024]{2,1,0:T(8,128)(2,1)}), bf16[8,16,1024]{2,1,0:T(8,128)(2,1)S(1)}, u32[]{:S(2)}, u32[]{:S(2)}) %all-to-all-start) | async-done | bytes 262176 | tf_op jit(solution)/shard_map/all_to_all | solution.py:58
  37.9 0.1 broadcast_in_dim.57
  38.0 11.2 %all_to_all.30 = bf16[4,128,1024]{2,1,0:T(8,128)(2,1)S(1)} all-to-all(bf16[4,128,1024]{2,1,0:T(8,128)(2,1)S(1)} %broadcast_in_dim.57), channel_id=1, replica_groups=mesh['zh'=8,'zl'=2,'xl'=2,'y'=4,'xh'=2,'c'=2] {'zl','xl'}, dimensions={0} | all-to-all | bytes 2097152 | tf_op jit(solution)/shard_map/all_to_all | solution.py:278
  49.3 1.5 %shard_map.48 = f32[16,48,128]{2,1,0:T(8,128)S(1)} custom-call(bf16[512,1024]{1,0:T(8,128)(2,1)S(1)} %bitcast.9, bf16[2,4,184,1024]{3,2,1,0:T(8,128)(2,1)S(1)} %shard_map.47.resp_ref), custom_call_target="tpu_custom_call" | custom-call | tf_op jit(solution)/shard_map/pallas_call | solution.py:281
  50.7 22.9 %all_to_all.31.parts_ref = f32[16,48,128]{2,1,0:T(8,128)S(1)} all-to-all(f32[16,48,128]{2,1,0:T(8,128)S(1)} %shard_map.48), channel_id=1, replica_groups=mesh['zh'=8,'zl'=2,'xl'=2,'y'=4,'xh'=2,'c'=2] {'y','xh','c'}, dimensions={0} | all-to-all | bytes 786432 | tf_op jit(solution)/shard_map/all_to_all | solution.py:289
  73.6 0.3 shard_map.49
  74.0 11.8 %all_to_all.32.win_ref = bf16[16,48,128]{2,1,0:T(8,128)(2,1)S(1)} all-to-all(bf16[16,48,128]{2,1,0:T(8,128)(2,1)S(1)} %shard_map.49), channel_id=1, replica_groups=mesh['zh'=8,'zl'=2,'xl'=2,'y'=4,'xh'=2,'c'=2] {'y','xh','c'}, dimensions={0} | all-to-all | bytes 393216 | tf_op jit(solution)/shard_map/all_to_all | solution.py:292
  85.8 1.2 shard_map.50
  86.9 15.3 %all_to_all.33.got_ref = bf16[4,128,1024]{2,1,0:T(8,128)(2,1)S(1)} all-to-all(bf16[4,128,1024]{2,1,0:T(8,128)(2,1)S(1)} %bitcast.10), channel_id=1, replica_groups=mesh['zh'=8,'zl'=2,'xl'=2,'y'=4,'xh'=2,'c'=2] {'zl','xl'}, dimensions={0} | all-to-all | bytes 2097152 | tf_op jit(solution)/shard_map/all_to_all | solution.py:302
  102.2 0.1 shard_map.51
  102.4 24.2 %all_to_all.34.got_ref = bf16[8,16,1024]{2,1,0:T(8,128)(2,1)S(1)} all-to-all(bf16[8,16,1024]{2,1,0:T(8,128)(2,1)S(1)} %bitcast.11), channel_id=1, replica_groups={{0,64,448,128,384,192,320,256},{1,65,449,129,385,193,321,257},{2,66,450..., dimensions={0} | all-to-all | bytes 524288 | tf_op jit(solution)/shard_map/all_to_all | solution.py:58
  126.6 6.9 %all_gather.11.sums_ref = f32[32,1024]{1,0:T(8,128)S(1)} all-gather(f32[16,1024]{1,0:T(8,128)S(1)} %shard_map.52), channel_id=1, replica_groups=mesh['zh'=8,'zl'=2,'xl'=2,'y'=4,'xh'=2,'c'=2] {'c'}, dimensions={0}, use_global_device_ids=true | all-gather | bytes 196608 | tf_op jit(solution)/shard_map/all_gather | solution.py:306
  133.5 1.3 shard_map.53
  (9 shorter events, 0.1 us)
Async XLA Ops:
  10.7 27.2 %all-to-all-start = ((bf16[8,16,1024]{2,1,0:T(8,128)(2,1)}), bf16[8,16,1024]{2,1,0:T(8,128)(2,1)S(1)}, u32[]{:S(2)}, u32[]{:S(2)}) async-start(bf16[8,16,1024]{2,1,0:T(8,128)(2,1)} %broadcast_in_dim.52), calls=%async_computation | async-start | bytes 524288 | tf_op jit(solution)/shard_map/all_to_all | solution.py:58
  20.9 1.9 %copy-start = (bf16[2,4,184,1024]{3,2,1,0:T(8,128)(2,1)S(1)}, bf16[2,4,184,1024]{3,2,1,0:T(8,128)(2,1)}, u32[]{:S(2)}) copy-start(bf16[2,4,184,1024]{3,2,1,0:T(8,128)(2,1)} %resp_ref.1) | copy-start | bytes 9043972
  22.8 0.7 copy-start.1

commit v9 on v6

--- a/solution.py
+++ b/solution.py
@@ -85,6 +85,17 @@
     other_ref[...] = sums[rows // 2 :]
 
 
+def near_body(own_ref, others_ref, out_ref, held_ref, sem_ref):
+    core = lax.axis_index("c")
+    held_ref[...] = (own_ref[...] + others_ref[1 - core]).astype(BF16)
+    copies = []
+    for j in range(out_ref.shape[0]):
+        copies.append(pltpu.make_async_copy(held_ref, out_ref.at[j], sem_ref.at[j]))
+        copies[-1].start()
+    for copy in copies:
+        copy.wait()
+
+
 def masked_body(band_ref, resp_ref, out_ref):
     band = band_ref[...].astype(F32).astype(BF16)
     down, across = band.shape
@@ -246,9 +257,14 @@
     )(f_time)
     others = lax.all_gather(other, "c", axis=0)
     others, core, gates, band_map = lax.optimization_barrier((others, core, gates, band_map))
-    other = jnp.where(core == 0, others[1], others[0])
-    spectra = (own + other).astype(BF16)
-    near = jnp.broadcast_to(spectra[None], (zh, own_rows, cols))
+    near = pl.pallas_call(
+        near_body,
+        out_shape=struct((zh, own_rows, cols), BF16),
+        in_specs=[pl.BlockSpec(memory_space=pltpu.VMEM)] * 2,
+        out_specs=pl.BlockSpec(memory_space=pltpu.HBM),
+        scratch_shapes=[pltpu.VMEM((own_rows, cols), BF16), pltpu.SemaphoreType.DMA((zh,))],
+        compiler_params=pltpu.CompilerParams(vmem_limit_bytes=12 << 20),
+    )(own, others)
     near = far_all_to_all(near).reshape(zh * own_rows, cols)
 
     masked = vmem_call(

time: 133 us -> 133 us (level)
  no operation moved by 1% of the time
where the time goes in v9:
time: 133 us; the launch traced here: 132 us
  blocking collectives  98.8 us (74%)
  waiting for transfers between devices  12.4 us (9%)
  starting transfers between devices  9.45 us (7%)
  Pallas kernels  7.26 us (5%)
  local copies, waits for them, and re-layouts  2.78 us (2%)
  matrix products  1.44 us (1%)
    all_to_all x1, blocking collectives, far_all_to_all(): return lax.all_to_all(x, axes, 0, 0, tiled=True, axis_index_groups=groups)  23.5 us
    all_to_all x1, blocking collectives, shards(): parts = lax.all_to_all(parts, RCV + ('c',), 0, 0, tiled=True)  19.9 us
    all_to_all x1, blocking collectives, shards(): lax.all_to_all(sends.reshape(pairs, zh * own_rows, cols), PAIR, 0, 0, til...  15.3 us
    all_to_all x1, blocking collectives, shards(): lax.all_to_all(every, PAIR, 0, 0, tiled=True).reshape(focal * ROWS, cols)  14.5 us
    all_to_all x1, waiting for transfers between devices, far_all_to_all(): return lax.all_to_all(x, axes, 0, 0, tiled=True, axis_index_groups=groups)  12.4 us
    all_to_all x1, blocking collectives, shards(): windowed = lax.all_to_all(gated, RCV + ('c',), 0, 0, tiled=True)  11.8 us
    all_to_all x1, starting transfers between devices, far_all_to_all(): return lax.all_to_all(x, axes, 0, 0, tiled=True, axis_index_groups=groups)  9.45 us
    all_gather x1, blocking collectives, shards(): others = lax.all_gather(other, 'c', axis=0)  8.42 us
  transfers between devices with their start and end apart: 1, of which 1 were waited for; matrix products, arithmetic and copies ran while one was open for 2% of the time, Pallas kernels for 0%

profile of v9, /device:TPU:1, one launch (start us, length us, event | category | flops | bytes accessed | tf_op | source)
XLA Modules:
  0.0 132.5 jit_solution(5414449536588113755)
XLA Ops:
  0.0 1.5 %shard_map.46 = (f32[16,1024]{1,0:T(8,128)S(1)}, f32[16,1024]{1,0:T(8,128)S(1)}, bf16[192,512]{1,0:T(8,128)(2,1)S(1)}) custom-call(bf16[256,2,1024]{2,1,0:T(2,128)(2,1)} %f_ref.1), custom_call_target="tpu_custom_call" | custom-call | tf_op jit(solution)/shard_map/pallas_call | solution.py:250
  1.5 8.4 %all-gather = f32[32,1024]{1,0:T(8,128)S(1)} all-gather(f32[16,1024]{1,0:T(8,128)S(1)} %get-tuple-element.17), channel_id=2, replica_groups=mesh['zh'=8,'zl'=2,'xl'=2,'y'=4,'xh'=2,'c'=2] {'c'}, dimensions={0}, use_global_device_ids=true | all-gather | bytes 196608 | tf_op jit(solution)/shard_map/all_gather | solution.py:258
  10.0 0.8 shard_map.47
  10.7 9.5 %all-to-all-start = ((bf16[8,16,1024]{2,1,0:T(8,128)(2,1)}), bf16[8,16,1024]{2,1,0:T(8,128)(2,1)S(1)}, u32[]{:S(2)}, u32[]{:S(2)}) async-start(bf16[8,16,1024]{2,1,0:T(8,128)(2,1)} %shard_map.47), calls=%async_computation | async-start | bytes 524288 | tf_op jit(solution)/shard_map/all_to_all | solution.py:59
  20.2 0.8 copy.5.band_ref
  21.0 0.0 copy-start
  21.0 1.9 %copy-done = bf16[2,4,184,1024]{3,2,1,0:T(8,128)(2,1)S(1)} copy-done((bf16[2,4,184,1024]{3,2,1,0:T(8,128)(2,1)S(1)}, bf16[2,4,184,1024]{3,2,1,0:T(8,128)(2,1)}, u32[]{:S(2)}) %copy-start) | copy-done | bytes 3014680
  22.8 0.6 shard_map.48.resp_ref
  23.5 0.0 copy-done.1
  23.5 0.3 select_reduce_fusion
  23.8 1.4 %convolution_select_fusion.matrix_ref = f32[64,64]{1,0:T(8,128)S(1)} fusion(s32[64]{0:T(128)S(1)} %get-tuple-element.31, s32[64]{0:T(128)S(1)} %get-tuple-element.35, s32[64]{0:T(128)S(1)} %get-tuple-element.32, s32[64]{0:T(128)S(1)} %get-tuple-element.34, s32[64]{0:T(128)S(1)} %get-tuple-element.33, s32[64]{0:T(128)S(1)} %get-tuple-element.36, ...), kind=kOutput, calls=%fused_computation | convolution fusion | flops 28614656 | bytes 18944 | tf_op jit(solution)/shard_map/dot_general | solution.py:287
  25.2 12.4 %all-to-all-done = bf16[8,16,1024]{2,1,0:T(8,128)(2,1)S(1)} async-done(((bf16[8,16,1024]{2,1,0:T(8,128)(2,1)}), bf16[8,16,1024]{2,1,0:T(8,128)(2,1)S(1)}, u32[]{:S(2)}, u32[]{:S(2)}) %all-to-all-start) | async-done | bytes 262176 | tf_op jit(solution)/shard_map/all_to_all | solution.py:59
  37.6 0.1 broadcast_in_dim.29
  37.7 14.5 %all_to_all.30 = bf16[4,128,1024]{2,1,0:T(8,128)(2,1)S(1)} all-to-all(bf16[4,128,1024]{2,1,0:T(8,128)(2,1)S(1)} %broadcast_in_dim.29), channel_id=1, replica_groups=mesh['zh'=8,'zl'=2,'xl'=2,'y'=4,'xh'=2,'c'=2] {'zl','xl'}, dimensions={0} | all-to-all | bytes 2097152 | tf_op jit(solution)/shard_map/all_to_all | solution.py:295
  52.2 1.5 %shard_map.49 = f32[16,48,128]{2,1,0:T(8,128)S(1)} custom-call(bf16[512,1024]{1,0:T(8,128)(2,1)S(1)} %bitcast.5, bf16[2,4,184,1024]{3,2,1,0:T(8,128)(2,1)S(1)} %shard_map.48.resp_ref), custom_call_target="tpu_custom_call" | custom-call | tf_op jit(solution)/shard_map/pallas_call | solution.py:298
  53.7 19.9 %all_to_all.31.parts_ref = f32[16,48,128]{2,1,0:T(8,128)S(1)} all-to-all(f32[16,48,128]{2,1,0:T(8,128)S(1)} %shard_map.49), channel_id=1, replica_groups=mesh['zh'=8,'zl'=2,'xl'=2,'y'=4,'xh'=2,'c'=2] {'y','xh','c'}, dimensions={0} | all-to-all | bytes 786432 | tf_op jit(solution)/shard_map/all_to_all | solution.py:306
  73.5 0.3 shard_map.50
  73.9 11.8 %all_to_all.32.win_ref = bf16[16,48,128]{2,1,0:T(8,128)(2,1)S(1)} all-to-all(bf16[16,48,128]{2,1,0:T(8,128)(2,1)S(1)} %shard_map.50), channel_id=1, replica_groups=mesh['zh'=8,'zl'=2,'xl'=2,'y'=4,'xh'=2,'c'=2] {'y','xh','c'}, dimensions={0} | all-to-all | bytes 393216 | tf_op jit(solution)/shard_map/all_to_all | solution.py:309
  85.7 1.2 shard_map.51
  86.9 15.3 %all_to_all.33.got_ref = bf16[4,128,1024]{2,1,0:T(8,128)(2,1)S(1)} all-to-all(bf16[4,128,1024]{2,1,0:T(8,128)(2,1)S(1)} %bitcast.6), channel_id=1, replica_groups=mesh['zh'=8,'zl'=2,'xl'=2,'y'=4,'xh'=2,'c'=2] {'zl','xl'}, dimensions={0} | all-to-all | bytes 2097152 | tf_op jit(solution)/shard_map/all_to_all | solution.py:319
  102.2 0.1 shard_map.52
  102.3 23.5 %all_to_all.34.got_ref = bf16[8,16,1024]{2,1,0:T(8,128)(2,1)S(1)} all-to-all(bf16[8,16,1024]{2,1,0:T(8,128)(2,1)S(1)} %bitcast.7), channel_id=1, replica_groups={{0,192,384,64,256,448,128,320},{1,193,385,65,257,449,129,321},{2,194,38..., dimensions={0} | all-to-all | bytes 524288 | tf_op jit(solution)/shard_map/all_to_all | solution.py:59
  125.8 5.4 %all_gather.11.sums_ref = f32[32,1024]{1,0:T(8,128)S(1)} all-gather(f32[16,1024]{1,0:T(8,128)S(1)} %shard_map.53), channel_id=1, replica_groups=mesh['zh'=8,'zl'=2,'xl'=2,'y'=4,'xh'=2,'c'=2] {'c'}, dimensions={0}, use_global_device_ids=true | all-gather | bytes 196608 | tf_op jit(solution)/shard_map/all_gather | solution.py:323
  131.2 1.3 shard_map.54
  (8 shorter events, 0.1 us)
Async XLA Ops:
  10.7 26.8 %all-to-all-start = ((bf16[8,16,1024]{2,1,0:T(8,128)(2,1)}), bf16[8,16,1024]{2,1,0:T(8,128)(2,1)S(1)}, u32[]{:S(2)}, u32[]{:S(2)}) async-start(bf16[8,16,1024]{2,1,0:T(8,128)(2,1)} %shard_map.47), calls=%async_computation | async-start | bytes 524288 | tf_op jit(solution)/shard_map/all_to_all | solution.py:59
  21.0 1.9 %copy-start = (bf16[2,4,184,1024]{3,2,1,0:T(8,128)(2,1)S(1)}, bf16[2,4,184,1024]{3,2,1,0:T(8,128)(2,1)}, u32[]{:S(2)}) copy-start(bf16[2,4,184,1024]{3,2,1,0:T(8,128)(2,1)} %resp_ref.1) | copy-start | bytes 9043972
  22.8 0.7 copy-start.1

commit v10 on v9

--- a/solution.py
+++ b/solution.py
@@ -47,8 +47,11 @@
 
 
 def far_order(count):
-    step = 1 if count % 3 == 0 else 3
-    return [step * j % count for j in range(count)]
+    order = list(range(count))
+    if count % 2 or count < 4:
+        return order
+    half = far_order(count // 2)
+    return [2 * j for j in half] + [2 * j + 1 for j in half]
 
 
 def far_all_to_all(x):
@@ -280,7 +283,7 @@
     waves = wave(row // part_rows * HALF + row % HALF, row // HALF % 2, col)
     point = (lax.axis_index(RCV) * 2 + core) * part_focal + iota((2 * part_rows, focal), 0) // ROWS % part_focal
     block = point // focal_here
-    far = block % zh * far_order(zh)[1] % zh
+    far = sum(jnp.where(block % zh == j, f, 0) for j, f in enumerate(far_order(zh)))
     point = (far * pairs + block // zh) * focal_here + point % focal_here
     window = jnp.where(point == iota((2 * part_rows, focal), 1), gates[None, :], 0).sum(1)
     inner = jnp.where(col < window[:, None], waves / math.sqrt(NT), 0.0)

time: 133 us -> 130 us (0.977); the launches traced: 132 us -> 128 us
  waiting for transfers between devices: 12.4 us -> 8.69 us
    all_to_all x1, blocking collectives: 23.5 us -> 19.8 us  [far_all_to_all(): return lax.all_to_all(x, axes, 0, 0, tiled=True, axis_index_groups=groups)]
    all_to_all x1, waiting for transfers between devices: 12.4 us -> 8.69 us  [far_all_to_all(): return lax.all_to_all(x, axes, 0, 0, tiled=True, axis_index_groups=groups)]
    all_to_all x1, blocking collectives: 14.5 us -> 17.3 us  [shards(): lax.all_to_all(every, PAIR, 0, 0, tiled=True).reshape(focal * ROWS, cols)]
where the time goes in v10:
time: 130 us; the launch traced here: 128 us
  blocking collectives  97.9 us (75%)
  starting transfers between devices  9.45 us (7%)
  waiting for transfers between devices  8.69 us (7%)
  Pallas kernels  7.26 us (6%)
  local copies, waits for them, and re-layouts  2.78 us (2%)
  matrix products  1.44 us (1%)
    all_to_all x1, blocking collectives, far_all_to_all(): return lax.all_to_all(x, axes, 0, 0, tiled=True, axis_index_groups=groups)  19.8 us
    all_to_all x1, blocking collectives, shards(): parts = lax.all_to_all(parts, RCV + ('c',), 0, 0, tiled=True)  19.3 us
    all_to_all x1, blocking collectives, shards(): lax.all_to_all(every, PAIR, 0, 0, tiled=True).reshape(focal * ROWS, cols)  17.3 us
    all_to_all x1, blocking collectives, shards(): lax.all_to_all(sends.reshape(pairs, zh * own_rows, cols), PAIR, 0, 0, til...  15.3 us
    all_to_all x1, blocking collectives, shards(): windowed = lax.all_to_all(gated, RCV + ('c',), 0, 0, tiled=True)  11.8 us
    all_to_all x1, starting transfers between devices, far_all_to_all(): return lax.all_to_all(x, axes, 0, 0, tiled=True, axis_index_groups=groups)  9.45 us
    all_to_all x1, waiting for transfers between devices, far_all_to_all(): return lax.all_to_all(x, axes, 0, 0, tiled=True, axis_index_groups=groups)  8.69 us
    all_gather x1, blocking collectives, shards(): others = lax.all_gather(other, 'c', axis=0)  8.42 us
  transfers between devices with their start and end apart: 1, of which 1 were waited for; matrix products, arithmetic and copies ran while one was open for 2% of the time, Pallas kernels for 0%

profile of v10, /device:TPU:1, one launch (start us, length us, event | category | flops | bytes accessed | tf_op | source)
XLA Modules:
  0.0 128.0 jit_solution(5783581344418562200)
XLA Ops:
  0.0 1.5 %shard_map.46 = (f32[16,1024]{1,0:T(8,128)S(1)}, f32[16,1024]{1,0:T(8,128)S(1)}, bf16[192,512]{1,0:T(8,128)(2,1)S(1)}) custom-call(bf16[256,2,1024]{2,1,0:T(2,128)(2,1)} %f_ref.1), custom_call_target="tpu_custom_call" | custom-call | tf_op jit(solution)/shard_map/pallas_call | solution.py:253
  1.5 8.4 %all-gather = f32[32,1024]{1,0:T(8,128)S(1)} all-gather(f32[16,1024]{1,0:T(8,128)S(1)} %get-tuple-element.17), channel_id=2, replica_groups=mesh['zh'=8,'zl'=2,'xl'=2,'y'=4,'xh'=2,'c'=2] {'c'}, dimensions={0}, use_global_device_ids=true | all-gather | bytes 196608 | tf_op jit(solution)/shard_map/all_gather | solution.py:261
  10.0 0.8 shard_map.47
  10.7 9.5 %all-to-all-start = ((bf16[8,16,1024]{2,1,0:T(8,128)(2,1)}), bf16[8,16,1024]{2,1,0:T(8,128)(2,1)S(1)}, u32[]{:S(2)}, u32[]{:S(2)}) async-start(bf16[8,16,1024]{2,1,0:T(8,128)(2,1)} %shard_map.47), calls=%async_computation | async-start | bytes 524288 | tf_op jit(solution)/shard_map/all_to_all | solution.py:62
  20.2 0.8 copy.5.band_ref
  21.0 0.0 copy-start
  21.0 1.9 %copy-done = bf16[2,4,184,1024]{3,2,1,0:T(8,128)(2,1)S(1)} copy-done((bf16[2,4,184,1024]{3,2,1,0:T(8,128)(2,1)S(1)}, bf16[2,4,184,1024]{3,2,1,0:T(8,128)(2,1)}, u32[]{:S(2)}) %copy-start) | copy-done | bytes 3014680
  22.8 0.6 shard_map.48.resp_ref
  23.5 0.0 copy-done.1
  23.5 0.3 select_reduce_fusion
  23.8 1.4 %convolution_select_fusion.matrix_ref = f32[64,64]{1,0:T(8,128)S(1)} fusion(s32[64]{0:T(128)S(1)} %get-tuple-element.31, s32[64]{0:T(128)S(1)} %get-tuple-element.35, s32[64]{0:T(128)S(1)} %get-tuple-element.32, s32[64]{0:T(128)S(1)} %get-tuple-element.34, s32[64]{0:T(128)S(1)} %get-tuple-element.33, s32[64]{0:T(128)S(1)} %get-tuple-element.36, ...), kind=kOutput, calls=%fused_computation | convolution fusion | flops 28614656 | bytes 18944 | tf_op jit(solution)/shard_map/dot_general | solution.py:290
  25.2 8.7 %all-to-all-done = bf16[8,16,1024]{2,1,0:T(8,128)(2,1)S(1)} async-done(((bf16[8,16,1024]{2,1,0:T(8,128)(2,1)}), bf16[8,16,1024]{2,1,0:T(8,128)(2,1)S(1)}, u32[]{:S(2)}, u32[]{:S(2)}) %all-to-all-start) | async-done | bytes 262176 | tf_op jit(solution)/shard_map/all_to_all | solution.py:62
  33.9 0.1 broadcast_in_dim.50
  34.0 17.3 %all_to_all.30 = bf16[4,128,1024]{2,1,0:T(8,128)(2,1)S(1)} all-to-all(bf16[4,128,1024]{2,1,0:T(8,128)(2,1)S(1)} %broadcast_in_dim.50), channel_id=1, replica_groups=mesh['zh'=8,'zl'=2,'xl'=2,'y'=4,'xh'=2,'c'=2] {'zl','xl'}, dimensions={0} | all-to-all | bytes 2097152 | tf_op jit(solution)/shard_map/all_to_all | solution.py:298
  51.3 1.5 %shard_map.49 = f32[16,48,128]{2,1,0:T(8,128)S(1)} custom-call(bf16[512,1024]{1,0:T(8,128)(2,1)S(1)} %bitcast.5, bf16[2,4,184,1024]{3,2,1,0:T(8,128)(2,1)S(1)} %shard_map.48.resp_ref), custom_call_target="tpu_custom_call" | custom-call | tf_op jit(solution)/shard_map/pallas_call | solution.py:301
  52.8 19.3 %all_to_all.31.parts_ref = f32[16,48,128]{2,1,0:T(8,128)S(1)} all-to-all(f32[16,48,128]{2,1,0:T(8,128)S(1)} %shard_map.49), channel_id=1, replica_groups=mesh['zh'=8,'zl'=2,'xl'=2,'y'=4,'xh'=2,'c'=2] {'y','xh','c'}, dimensions={0} | all-to-all | bytes 786432 | tf_op jit(solution)/shard_map/all_to_all | solution.py:309
  72.1 0.3 shard_map.50
  72.4 11.8 %all_to_all.32.win_ref = bf16[16,48,128]{2,1,0:T(8,128)(2,1)S(1)} all-to-all(bf16[16,48,128]{2,1,0:T(8,128)(2,1)S(1)} %shard_map.50), channel_id=1, replica_groups=mesh['zh'=8,'zl'=2,'xl'=2,'y'=4,'xh'=2,'c'=2] {'y','xh','c'}, dimensions={0} | all-to-all | bytes 393216 | tf_op jit(solution)/shard_map/all_to_all | solution.py:312
  84.2 1.2 shard_map.51
  85.4 15.3 %all_to_all.33.got_ref = bf16[4,128,1024]{2,1,0:T(8,128)(2,1)S(1)} all-to-all(bf16[4,128,1024]{2,1,0:T(8,128)(2,1)S(1)} %bitcast.6), channel_id=1, replica_groups=mesh['zh'=8,'zl'=2,'xl'=2,'y'=4,'xh'=2,'c'=2] {'zl','xl'}, dimensions={0} | all-to-all | bytes 2097152 | tf_op jit(solution)/shard_map/all_to_all | solution.py:322
  100.7 0.1 shard_map.52
  100.8 19.8 %all_to_all.34.got_ref = bf16[8,16,1024]{2,1,0:T(8,128)(2,1)S(1)} all-to-all(bf16[8,16,1024]{2,1,0:T(8,128)(2,1)S(1)} %bitcast.7), channel_id=1, replica_groups={{0,256,128,384,64,320,192,448},{1,257,129,385,65,321,193,449},{2,258,13..., dimensions={0} | all-to-all | bytes 524288 | tf_op jit(solution)/shard_map/all_to_all | solution.py:62
  120.6 6.1 %all_gather.11.sums_ref = f32[32,1024]{1,0:T(8,128)S(1)} all-gather(f32[16,1024]{1,0:T(8,128)S(1)} %shard_map.53), channel_id=1, replica_groups=mesh['zh'=8,'zl'=2,'xl'=2,'y'=4,'xh'=2,'c'=2] {'c'}, dimensions={0}, use_global_device_ids=true | all-gather | bytes 196608 | tf_op jit(solution)/shard_map/all_gather | solution.py:326
  126.7 1.3 shard_map.54
  (8 shorter events, 0.1 us)
Async XLA Ops:
  10.7 23.2 %all-to-all-start = ((bf16[8,16,1024]{2,1,0:T(8,128)(2,1)}), bf16[8,16,1024]{2,1,0:T(8,128)(2,1)S(1)}, u32[]{:S(2)}, u32[]{:S(2)}) async-start(bf16[8,16,1024]{2,1,0:T(8,128)(2,1)} %shard_map.47), calls=%async_computation | async-start | bytes 524288 | tf_op jit(solution)/shard_map/all_to_all | solution.py:62
  21.0 1.9 %copy-start = (bf16[2,4,184,1024]{3,2,1,0:T(8,128)(2,1)S(1)}, bf16[2,4,184,1024]{3,2,1,0:T(8,128)(2,1)}, u32[]{:S(2)}) copy-start(bf16[2,4,184,1024]{3,2,1,0:T(8,128)(2,1)} %resp_ref.1) | copy-start | bytes 9043972
  22.8 0.7 copy-start.1

commit v11 on v9

--- a/solution.py
+++ b/solution.py
@@ -47,8 +47,9 @@
 
 
 def far_order(count):
-    step = 1 if count % 3 == 0 else 3
-    return [step * j % count for j in range(count)]
+    half = count // 2
+    order = [j for i in range(half) for j in (i, i + half)]
+    return order + list(range(2 * half, count))
 
 
 def far_all_to_all(x):
@@ -280,7 +281,7 @@
     waves = wave(row // part_rows * HALF + row % HALF, row // HALF % 2, col)
     point = (lax.axis_index(RCV) * 2 + core) * part_focal + iota((2 * part_rows, focal), 0) // ROWS % part_focal
     block = point // focal_here
-    far = block % zh * far_order(zh)[1] % zh
+    far = sum(jnp.where(block % zh == j, f, 0) for j, f in enumerate(far_order(zh)))
     point = (far * pairs + block // zh) * focal_here + point % focal_here
     window = jnp.where(point == iota((2 * part_rows, focal), 1), gates[None, :], 0).sum(1)
     inner = jnp.where(col < window[:, None], waves / math.sqrt(NT), 0.0)

time: 133 us -> 131 us (0.985); the launches traced: 132 us -> 129 us
  waiting for transfers between devices: 12.4 us -> 8.97 us
    all_to_all x1, blocking collectives: 23.5 us -> 19.6 us  [far_all_to_all(): return lax.all_to_all(x, axes, 0, 0, tiled=True, axis_index_groups=groups)]
    all_to_all x1, waiting for transfers between devices: 12.4 us -> 8.97 us  [far_all_to_all(): return lax.all_to_all(x, axes, 0, 0, tiled=True, axis_index_groups=groups)]
    all_to_all x1, blocking collectives: 14.5 us -> 16.6 us  [shards(): lax.all_to_all(every, PAIR, 0, 0, tiled=True).reshape(focal * ROWS, cols)]
    all_gather x1, blocking collectives: 5.37 us -> 6.77 us  [shards(): both = lax.all_gather(got, 'c', axis=0, tiled=True)]
where the time goes in v11:
time: 131 us; the launch traced here: 129 us
  blocking collectives  98.3 us (75%)
  starting transfers between devices  9.45 us (7%)
  waiting for transfers between devices  8.97 us (7%)
  Pallas kernels  7.28 us (6%)
  local copies, waits for them, and re-layouts  2.78 us (2%)
  matrix products  1.44 us (1%)
    all_to_all x1, blocking collectives, shards(): parts = lax.all_to_all(parts, RCV + ('c',), 0, 0, tiled=True)  19.9 us
    all_to_all x1, blocking collectives, far_all_to_all(): return lax.all_to_all(x, axes, 0, 0, tiled=True, axis_index_groups=groups)  19.6 us
    all_to_all x1, blocking collectives, shards(): lax.all_to_all(every, PAIR, 0, 0, tiled=True).reshape(focal * ROWS, cols)  16.6 us
    all_to_all x1, blocking collectives, shards(): lax.all_to_all(sends.reshape(pairs, zh * own_rows, cols), PAIR, 0, 0, til...  15.3 us
    all_to_all x1, blocking collectives, shards(): windowed = lax.all_to_all(gated, RCV + ('c',), 0, 0, tiled=True)  11.8 us
    all_to_all x1, starting transfers between devices, far_all_to_all(): return lax.all_to_all(x, axes, 0, 0, tiled=True, axis_index_groups=groups)  9.45 us
    all_to_all x1, waiting for transfers between devices, far_all_to_all(): return lax.all_to_all(x, axes, 0, 0, tiled=True, axis_index_groups=groups)  8.97 us
    all_gather x1, blocking collectives, shards(): others = lax.all_gather(other, 'c', axis=0)  8.42 us
  transfers between devices with their start and end apart: 1, of which 1 were waited for; matrix products, arithmetic and copies ran while one was open for 2% of the time, Pallas kernels for 0%

profile of v11, /device:TPU:1, one launch (start us, length us, event | category | flops | bytes accessed | tf_op | source)
XLA Modules:
  0.0 128.7 jit_solution(3702757084040177022)
XLA Ops:
  0.0 1.5 %shard_map.46 = (f32[16,1024]{1,0:T(8,128)S(1)}, f32[16,1024]{1,0:T(8,128)S(1)}, bf16[192,512]{1,0:T(8,128)(2,1)S(1)}) custom-call(bf16[256,2,1024]{2,1,0:T(2,128)(2,1)} %f_ref.1), custom_call_target="tpu_custom_call" | custom-call | tf_op jit(solution)/shard_map/pallas_call | solution.py:251
  1.5 8.4 %all-gather = f32[32,1024]{1,0:T(8,128)S(1)} all-gather(f32[16,1024]{1,0:T(8,128)S(1)} %get-tuple-element.17), channel_id=2, replica_groups=mesh['zh'=8,'zl'=2,'xl'=2,'y'=4,'xh'=2,'c'=2] {'c'}, dimensions={0}, use_global_device_ids=true | all-gather | bytes 196608 | tf_op jit(solution)/shard_map/all_gather | solution.py:259
  10.0 0.8 shard_map.47
  10.7 9.5 %all-to-all-start = ((bf16[8,16,1024]{2,1,0:T(8,128)(2,1)}), bf16[8,16,1024]{2,1,0:T(8,128)(2,1)S(1)}, u32[]{:S(2)}, u32[]{:S(2)}) async-start(bf16[8,16,1024]{2,1,0:T(8,128)(2,1)} %shard_map.47), calls=%async_computation | async-start | bytes 524288 | tf_op jit(solution)/shard_map/all_to_all | solution.py:60
  20.2 0.8 copy.5.band_ref
  21.0 0.0 copy-start
  21.0 1.9 %copy-done = bf16[2,4,184,1024]{3,2,1,0:T(8,128)(2,1)S(1)} copy-done((bf16[2,4,184,1024]{3,2,1,0:T(8,128)(2,1)S(1)}, bf16[2,4,184,1024]{3,2,1,0:T(8,128)(2,1)}, u32[]{:S(2)}) %copy-start) | copy-done | bytes 3014680
  22.8 0.6 shard_map.48.resp_ref
  23.5 0.0 copy-done.1
  23.5 0.3 select_reduce_fusion
  23.8 1.4 %convolution_select_fusion.matrix_ref = f32[64,64]{1,0:T(8,128)S(1)} fusion(s32[64]{0:T(128)S(1)} %get-tuple-element.31, s32[64]{0:T(128)S(1)} %get-tuple-element.35, s32[64]{0:T(128)S(1)} %get-tuple-element.32, s32[64]{0:T(128)S(1)} %get-tuple-element.34, s32[64]{0:T(128)S(1)} %get-tuple-element.33, s32[64]{0:T(128)S(1)} %get-tuple-element.36, ...), kind=kOutput, calls=%fused_computation | convolution fusion | flops 28614656 | bytes 18944 | tf_op jit(solution)/shard_map/dot_general | solution.py:288
  25.2 9.0 %all-to-all-done = bf16[8,16,1024]{2,1,0:T(8,128)(2,1)S(1)} async-done(((bf16[8,16,1024]{2,1,0:T(8,128)(2,1)}), bf16[8,16,1024]{2,1,0:T(8,128)(2,1)S(1)}, u32[]{:S(2)}, u32[]{:S(2)}) %all-to-all-start) | async-done | bytes 262176 | tf_op jit(solution)/shard_map/all_to_all | solution.py:60
  34.2 0.1 broadcast_in_dim.53
  34.3 16.6 %all_to_all.30 = bf16[4,128,1024]{2,1,0:T(8,128)(2,1)S(1)} all-to-all(bf16[4,128,1024]{2,1,0:T(8,128)(2,1)S(1)} %broadcast_in_dim.53), channel_id=1, replica_groups=mesh['zh'=8,'zl'=2,'xl'=2,'y'=4,'xh'=2,'c'=2] {'zl','xl'}, dimensions={0} | all-to-all | bytes 2097152 | tf_op jit(solution)/shard_map/all_to_all | solution.py:296
  50.9 1.5 %shard_map.49 = f32[16,48,128]{2,1,0:T(8,128)S(1)} custom-call(bf16[512,1024]{1,0:T(8,128)(2,1)S(1)} %bitcast.5, bf16[2,4,184,1024]{3,2,1,0:T(8,128)(2,1)S(1)} %shard_map.48.resp_ref), custom_call_target="tpu_custom_call" | custom-call | tf_op jit(solution)/shard_map/pallas_call | solution.py:299
  52.4 19.9 %all_to_all.31.parts_ref = f32[16,48,128]{2,1,0:T(8,128)S(1)} all-to-all(f32[16,48,128]{2,1,0:T(8,128)S(1)} %shard_map.49), channel_id=1, replica_groups=mesh['zh'=8,'zl'=2,'xl'=2,'y'=4,'xh'=2,'c'=2] {'y','xh','c'}, dimensions={0} | all-to-all | bytes 786432 | tf_op jit(solution)/shard_map/all_to_all | solution.py:307
  72.3 0.3 shard_map.50
  72.6 11.8 %all_to_all.32.win_ref = bf16[16,48,128]{2,1,0:T(8,128)(2,1)S(1)} all-to-all(bf16[16,48,128]{2,1,0:T(8,128)(2,1)S(1)} %shard_map.50), channel_id=1, replica_groups=mesh['zh'=8,'zl'=2,'xl'=2,'y'=4,'xh'=2,'c'=2] {'y','xh','c'}, dimensions={0} | all-to-all | bytes 393216 | tf_op jit(solution)/shard_map/all_to_all | solution.py:310
  84.4 1.2 shard_map.51
  85.6 15.3 %all_to_all.33.got_ref = bf16[4,128,1024]{2,1,0:T(8,128)(2,1)S(1)} all-to-all(bf16[4,128,1024]{2,1,0:T(8,128)(2,1)S(1)} %bitcast.6), channel_id=1, replica_groups=mesh['zh'=8,'zl'=2,'xl'=2,'y'=4,'xh'=2,'c'=2] {'zl','xl'}, dimensions={0} | all-to-all | bytes 2097152 | tf_op jit(solution)/shard_map/all_to_all | solution.py:320
  100.9 0.1 shard_map.52
  101.0 19.6 %all_to_all.34.got_ref = bf16[8,16,1024]{2,1,0:T(8,128)(2,1)S(1)} all-to-all(bf16[8,16,1024]{2,1,0:T(8,128)(2,1)S(1)} %bitcast.7), channel_id=1, replica_groups={{0,256,64,320,128,384,192,448},{1,257,65,321,129,385,193,449},{2,258,66..., dimensions={0} | all-to-all | bytes 524288 | tf_op jit(solution)/shard_map/all_to_all | solution.py:60
  120.6 6.8 %all_gather.11.sums_ref = f32[32,1024]{1,0:T(8,128)S(1)} all-gather(f32[16,1024]{1,0:T(8,128)S(1)} %shard_map.53), channel_id=1, replica_groups=mesh['zh'=8,'zl'=2,'xl'=2,'y'=4,'xh'=2,'c'=2] {'c'}, dimensions={0}, use_global_device_ids=true | all-gather | bytes 196608 | tf_op jit(solution)/shard_map/all_gather | solution.py:324
  127.4 1.3 shard_map.54
  (8 shorter events, 0.1 us)
Async XLA Ops:
  10.7 23.4 %all-to-all-start = ((bf16[8,16,1024]{2,1,0:T(8,128)(2,1)}), bf16[8,16,1024]{2,1,0:T(8,128)(2,1)S(1)}, u32[]{:S(2)}, u32[]{:S(2)}) async-start(bf16[8,16,1024]{2,1,0:T(8,128)(2,1)} %shard_map.47), calls=%async_computation | async-start | bytes 524288 | tf_op jit(solution)/shard_map/all_to_all | solution.py:60
  21.0 1.9 %copy-start = (bf16[2,4,184,1024]{3,2,1,0:T(8,128)(2,1)S(1)}, bf16[2,4,184,1024]{3,2,1,0:T(8,128)(2,1)}, u32[]{:S(2)}) copy-start(bf16[2,4,184,1024]{3,2,1,0:T(8,128)(2,1)} %resp_ref.1) | copy-start | bytes 9043972
  22.8 0.7 copy-start.1

commit v12 on v10

--- a/solution.py
+++ b/solution.py
@@ -51,7 +51,8 @@
     if count % 2 or count < 4:
         return order
     half = far_order(count // 2)
-    return [2 * j for j in half] + [2 * j + 1 for j in half]
+    turn = half[len(half) // 2 :] + half[: len(half) // 2]
+    return [2 * j for j in half] + [2 * j + 1 for j in turn]
 
 
 def far_all_to_all(x):

time: 130 us -> 133 us (1.023)
  blocking collectives: 97.9 us -> 100 us
  waiting for transfers between devices: 8.69 us -> 10.3 us
    all_gather x1, blocking collectives: 6.13 us -> 9.52 us  [shards(): both = lax.all_gather(got, 'c', axis=0, tiled=True)]
    all_to_all x1, waiting for transfers between devices: 8.69 us -> 10.3 us  [far_all_to_all(): return lax.all_to_all(x, axes, 0, 0, tiled=True, axis_index_groups=groups)]
    all_to_all x1, blocking collectives: 19.8 us -> 18.4 us  [far_all_to_all(): return lax.all_to_all(x, axes, 0, 0, tiled=True, axis_index_groups=groups)]
where the time goes in v12:
time: 133 us; the launch traced here: 132 us
  blocking collectives  100 us (75%)
  waiting for transfers between devices  10.3 us (8%)
  starting transfers between devices  9.45 us (7%)
  Pallas kernels  7.27 us (5%)
  local copies, waits for them, and re-layouts  2.78 us (2%)
  matrix products  1.44 us (1%)
    all_to_all x1, blocking collectives, shards(): parts = lax.all_to_all(parts, RCV + ('c',), 0, 0, tiled=True)  19.7 us
    all_to_all x1, blocking collectives, far_all_to_all(): return lax.all_to_all(x, axes, 0, 0, tiled=True, axis_index_groups=groups)  18.4 us
    all_to_all x1, blocking collectives, shards(): lax.all_to_all(every, PAIR, 0, 0, tiled=True).reshape(focal * ROWS, cols)  17.3 us
    all_to_all x1, blocking collectives, shards(): lax.all_to_all(sends.reshape(pairs, zh * own_rows, cols), PAIR, 0, 0, til...  15.3 us
    all_to_all x1, blocking collectives, shards(): windowed = lax.all_to_all(gated, RCV + ('c',), 0, 0, tiled=True)  11.8 us
    all_to_all x1, waiting for transfers between devices, far_all_to_all(): return lax.all_to_all(x, axes, 0, 0, tiled=True, axis_index_groups=groups)  10.3 us
    all_gather x1, blocking collectives, shards(): both = lax.all_gather(got, 'c', axis=0, tiled=True)  9.52 us
    all_to_all x1, starting transfers between devices, far_all_to_all(): return lax.all_to_all(x, axes, 0, 0, tiled=True, axis_index_groups=groups)  9.45 us
  transfers between devices with their start and end apart: 1, of which 1 were waited for; matrix products, arithmetic and copies ran while one was open for 2% of the time, Pallas kernels for 0%

profile of v12, /device:TPU:1, one launch (start us, length us, event | category | flops | bytes accessed | tf_op | source)
XLA Modules:
  0.0 132.1 jit_solution(11531186668927087283)
XLA Ops:
  0.0 1.5 %shard_map.46 = (f32[16,1024]{1,0:T(8,128)S(1)}, f32[16,1024]{1,0:T(8,128)S(1)}, bf16[192,512]{1,0:T(8,128)(2,1)S(1)}) custom-call(bf16[256,2,1024]{2,1,0:T(2,128)(2,1)} %f_ref.1), custom_call_target="tpu_custom_call" | custom-call | tf_op jit(solution)/shard_map/pallas_call | solution.py:254
  1.5 8.4 %all-gather = f32[32,1024]{1,0:T(8,128)S(1)} all-gather(f32[16,1024]{1,0:T(8,128)S(1)} %get-tuple-element.17), channel_id=2, replica_groups=mesh['zh'=8,'zl'=2,'xl'=2,'y'=4,'xh'=2,'c'=2] {'c'}, dimensions={0}, use_global_device_ids=true | all-gather | bytes 196608 | tf_op jit(solution)/shard_map/all_gather | solution.py:262
  10.0 0.8 shard_map.47
  10.7 9.5 %all-to-all-start = ((bf16[8,16,1024]{2,1,0:T(8,128)(2,1)}), bf16[8,16,1024]{2,1,0:T(8,128)(2,1)S(1)}, u32[]{:S(2)}, u32[]{:S(2)}) async-start(bf16[8,16,1024]{2,1,0:T(8,128)(2,1)} %shard_map.47), calls=%async_computation | async-start | bytes 524288 | tf_op jit(solution)/shard_map/all_to_all | solution.py:63
  20.2 0.8 copy.5.band_ref
  21.0 0.0 copy-start
  21.0 1.9 %copy-done = bf16[2,4,184,1024]{3,2,1,0:T(8,128)(2,1)S(1)} copy-done((bf16[2,4,184,1024]{3,2,1,0:T(8,128)(2,1)S(1)}, bf16[2,4,184,1024]{3,2,1,0:T(8,128)(2,1)}, u32[]{:S(2)}) %copy-start) | copy-done | bytes 3014680
  22.8 0.6 shard_map.48.resp_ref
  23.5 0.0 copy-done.1
  23.5 0.3 select_reduce_fusion
  23.8 1.4 %convolution_select_fusion.matrix_ref = f32[64,64]{1,0:T(8,128)S(1)} fusion(s32[64]{0:T(128)S(1)} %get-tuple-element.31, s32[64]{0:T(128)S(1)} %get-tuple-element.35, s32[64]{0:T(128)S(1)} %get-tuple-element.32, s32[64]{0:T(128)S(1)} %get-tuple-element.34, s32[64]{0:T(128)S(1)} %get-tuple-element.33, s32[64]{0:T(128)S(1)} %get-tuple-element.36, ...), kind=kOutput, calls=%fused_computation | convolution fusion | flops 28614656 | bytes 18944 | tf_op jit(solution)/shard_map/dot_general | solution.py:291
  25.2 10.3 %all-to-all-done = bf16[8,16,1024]{2,1,0:T(8,128)(2,1)S(1)} async-done(((bf16[8,16,1024]{2,1,0:T(8,128)(2,1)}), bf16[8,16,1024]{2,1,0:T(8,128)(2,1)S(1)}, u32[]{:S(2)}, u32[]{:S(2)}) %all-to-all-start) | async-done | bytes 262176 | tf_op jit(solution)/shard_map/all_to_all | solution.py:63
  35.5 0.1 broadcast_in_dim.50
  35.6 17.3 %all_to_all.30 = bf16[4,128,1024]{2,1,0:T(8,128)(2,1)S(1)} all-to-all(bf16[4,128,1024]{2,1,0:T(8,128)(2,1)S(1)} %broadcast_in_dim.50), channel_id=1, replica_groups=mesh['zh'=8,'zl'=2,'xl'=2,'y'=4,'xh'=2,'c'=2] {'zl','xl'}, dimensions={0} | all-to-all | bytes 2097152 | tf_op jit(solution)/shard_map/all_to_all | solution.py:299
  52.9 1.5 %shard_map.49 = f32[16,48,128]{2,1,0:T(8,128)S(1)} custom-call(bf16[512,1024]{1,0:T(8,128)(2,1)S(1)} %bitcast.5, bf16[2,4,184,1024]{3,2,1,0:T(8,128)(2,1)S(1)} %shard_map.48.resp_ref), custom_call_target="tpu_custom_call" | custom-call | tf_op jit(solution)/shard_map/pallas_call | solution.py:302
  54.4 19.7 %all_to_all.31.parts_ref = f32[16,48,128]{2,1,0:T(8,128)S(1)} all-to-all(f32[16,48,128]{2,1,0:T(8,128)S(1)} %shard_map.49), channel_id=1, replica_groups=mesh['zh'=8,'zl'=2,'xl'=2,'y'=4,'xh'=2,'c'=2] {'y','xh','c'}, dimensions={0} | all-to-all | bytes 786432 | tf_op jit(solution)/shard_map/all_to_all | solution.py:310
  74.1 0.3 shard_map.50
  74.5 11.8 %all_to_all.32.win_ref = bf16[16,48,128]{2,1,0:T(8,128)(2,1)S(1)} all-to-all(bf16[16,48,128]{2,1,0:T(8,128)(2,1)S(1)} %shard_map.50), channel_id=1, replica_groups=mesh['zh'=8,'zl'=2,'xl'=2,'y'=4,'xh'=2,'c'=2] {'y','xh','c'}, dimensions={0} | all-to-all | bytes 393216 | tf_op jit(solution)/shard_map/all_to_all | solution.py:313
  86.3 1.2 shard_map.51
  87.5 15.3 %all_to_all.33.got_ref = bf16[4,128,1024]{2,1,0:T(8,128)(2,1)S(1)} all-to-all(bf16[4,128,1024]{2,1,0:T(8,128)(2,1)S(1)} %bitcast.6), channel_id=1, replica_groups=mesh['zh'=8,'zl'=2,'xl'=2,'y'=4,'xh'=2,'c'=2] {'zl','xl'}, dimensions={0} | all-to-all | bytes 2097152 | tf_op jit(solution)/shard_map/all_to_all | solution.py:323
  102.8 0.1 shard_map.52
  102.9 18.4 %all_to_all.34.got_ref = bf16[8,16,1024]{2,1,0:T(8,128)(2,1)S(1)} all-to-all(bf16[8,16,1024]{2,1,0:T(8,128)(2,1)S(1)} %bitcast.7), channel_id=1, replica_groups={{0,256,384,128,448,192,64,320},{1,257,385,129,449,193,65,321},{2,258,38..., dimensions={0} | all-to-all | bytes 524288 | tf_op jit(solution)/shard_map/all_to_all | solution.py:63
  121.3 9.5 %all_gather.11.sums_ref = f32[32,1024]{1,0:T(8,128)S(1)} all-gather(f32[16,1024]{1,0:T(8,128)S(1)} %shard_map.53), channel_id=1, replica_groups=mesh['zh'=8,'zl'=2,'xl'=2,'y'=4,'xh'=2,'c'=2] {'c'}, dimensions={0}, use_global_device_ids=true | all-gather | bytes 196608 | tf_op jit(solution)/shard_map/all_gather | solution.py:327
  130.8 1.3 shard_map.54
  (8 shorter events, 0.1 us)
Async XLA Ops:
  10.7 24.7 %all-to-all-start = ((bf16[8,16,1024]{2,1,0:T(8,128)(2,1)}), bf16[8,16,1024]{2,1,0:T(8,128)(2,1)S(1)}, u32[]{:S(2)}, u32[]{:S(2)}) async-start(bf16[8,16,1024]{2,1,0:T(8,128)(2,1)} %shard_map.47), calls=%async_computation | async-start | bytes 524288 | tf_op jit(solution)/shard_map/all_to_all | solution.py:63
  21.0 1.9 %copy-start = (bf16[2,4,184,1024]{3,2,1,0:T(8,128)(2,1)S(1)}, bf16[2,4,184,1024]{3,2,1,0:T(8,128)(2,1)}, u32[]{:S(2)}) copy-start(bf16[2,4,184,1024]{3,2,1,0:T(8,128)(2,1)} %resp_ref.1) | copy-start | bytes 9043972
  22.8 0.7 copy-start.1
